TPU v7x, 512 devices: a whole 4x8x8 slice. The times are simulated.
512 devices in a mesh: energy: 32 (over x, z_hi, core), cuts: 16 (over z_lo, y).
Axes of the slice: x: 4, y: 8, z: 8 (z_hi: 4, z_lo: 2; z = z_hi * 2 + z_lo), core: 2. Of those that a mesh axis runs over, the one named last changes fastest.
Arguments:
- green_diag: bfloat16 [16, 128, 2, 256, 256], P('cuts', 'energy'), may hold values from -0.375 to 0.375
- green_upper: bfloat16 [16, 128, 2, 256, 256], P('cuts', 'energy'), may hold values from -0.375 to 0.375
- sigma_lesser: bfloat16 [16, 128, 2, 256, 256], P('cuts', 'energy'), may hold values from -6 to 6
- screening: bfloat16 [16, 128, 2, 256, 256], P('cuts', 'energy'), may hold values from -0.375 to 0.375
Outputs:
- polar_screened: bfloat16 [16, 128, 2, 256, 256], P('cuts', 'energy')
All inputs are finite; a program needn't handle non-finite values.
Results may differ from a plain program's by a relative error of at most 0.013.
Values may be sent and summed in bfloat16 or wider, within the bound.
No kernel may reach another device: no remote copies, remote signals or barrier semaphores. Data moves between devices by JAX's collectives and lax.ppermute only.
A program may use at most 64 MiB of HBM per device.

v0:
```python
import math

import jax
import jax.numpy as jnp
from jax import lax
from jax.sharding import PartitionSpec as P


def shifted(value, axis, steps):
    count = lax.axis_size(axis)
    leading, last = (max(0, -steps), min(count, count - steps))
    return lax.ppermute(value, axis, [(source, source + steps) for source in range(leading, last)])


def times_block(left, right):
    real = jnp.einsum(
        "eij,ejk->eik", left[:, 0], right[:, 0], preferred_element_type=jnp.float32
    ) - jnp.einsum("eij,ejk->eik", left[:, 1], right[:, 1], preferred_element_type=jnp.float32)
    imag = jnp.einsum(
        "eij,ejk->eik", left[:, 0], right[:, 1], preferred_element_type=jnp.float32
    ) + jnp.einsum("eij,ejk->eik", left[:, 1], right[:, 0], preferred_element_type=jnp.float32)
    return jnp.stack([real, imag], axis=1)


def times_adjoint(left, right):
    real = jnp.einsum(
        "eij,ekj->eik", left[:, 0], right[:, 0], preferred_element_type=jnp.float32
    ) + jnp.einsum("eij,ekj->eik", left[:, 1], right[:, 1], preferred_element_type=jnp.float32)
    imag = jnp.einsum(
        "eij,ekj->eik", left[:, 1], right[:, 0], preferred_element_type=jnp.float32
    ) - jnp.einsum("eij,ekj->eik", left[:, 0], right[:, 1], preferred_element_type=jnp.float32)
    return jnp.stack([real, imag], axis=1)


def angle_table(rows_count, cols_count, period):
    row_index = lax.broadcasted_iota(jnp.int32, (rows_count, cols_count), 0)
    col_index = lax.broadcasted_iota(jnp.int32, (rows_count, cols_count), 1)
    phase = (row_index * col_index % period).astype(jnp.float32)
    return phase * (2.0 * math.pi / period)


def split_table_dot(table, data):
    upper = table.astype(jnp.bfloat16)
    lower = (table - upper.astype(jnp.float32)).astype(jnp.bfloat16)
    return jnp.dot(upper, data, preferred_element_type=jnp.float32) + jnp.dot(
        lower, data, preferred_element_type=jnp.float32
    )


def correlate(spread):
    energies = spread.shape[0]
    period = 2 * energies
    forward = angle_table(period, energies, period)
    inverse = angle_table(energies, period, period)
    cos_inv = jnp.cos(inverse)
    sin_inv = jnp.sin(inverse)
    real_part = spread[:, 0].reshape(energies, -1)
    imag_part = spread[:, 1].reshape(energies, -1)
    width = real_part.shape[1]
    joined = jnp.concatenate([real_part, imag_part], axis=1)
    cos_both = split_table_dot(jnp.cos(forward), joined)
    sin_both = split_table_dot(jnp.sin(forward), joined)
    spec_real = cos_both[:, :width] + sin_both[:, width:]
    spec_imag = cos_both[:, width:] - sin_both[:, :width]
    power = spec_real * spec_real + spec_imag * spec_imag
    lag_real = jnp.dot(cos_inv, power) / period
    lag_imag = jnp.dot(sin_inv, power) / period
    polar = jnp.stack([lag_real, lag_imag], axis=1) / energies
    return polar.reshape(spread.shape).astype(jnp.bfloat16)


def shards(green_diag, green_upper, sigma_lesser, screening):
    sigma_next = shifted(sigma_lesser, "cuts", -1)
    own_term = times_block(green_diag[0], sigma_lesser[0]).astype(jnp.bfloat16)
    pair_term = times_block(green_upper[0], sigma_next[0]).astype(jnp.bfloat16)
    lesser = (
        times_adjoint(own_term, green_diag[0]) + times_adjoint(pair_term, green_upper[0])
    ).astype(jnp.bfloat16)
    entries = lax.all_to_all(lesser, "energy", split_axis=2, concat_axis=0, tiled=True)
    polar_rows = correlate(entries)
    back_field = lax.all_to_all(polar_rows, "energy", split_axis=0, concat_axis=2, tiled=True)
    screened_left = times_block(screening[0], back_field).astype(jnp.bfloat16)
    result_field = times_adjoint(screened_left, screening[0]).astype(jnp.bfloat16)
    return result_field[None]


def solution(mesh):
    in_specs = (
        P("cuts", "energy", None, None, None),
        P("cuts", "energy", None, None, None),
        P("cuts", "energy", None, None, None),
        P("cuts", "energy", None, None, None),
    )
    out_specs = P("cuts", "energy", None, None, None)
    return jax.shard_map(shards, mesh=mesh, in_specs=in_specs, out_specs=out_specs, check_vma=False)
```

profile of v0, /device:TPU:57, one launch (start us, length us, event | category | flops | bytes accessed | tf_op | source)
XLA Modules:
  0.0 122.9 jit_solution(17262940203430919250)
XLA Ops:
  0.0 1.4 %copy.101 = bf16[1,4,2,256,256]{4,3,1,2,0:T(8,128)(2,1)S(1)} copy(bf16[1,4,2,256,256]{4,3,2,1,0:T(8,128)(2,1)} %param.6) | data formatting | bytes 2097152 | tf_op args[2]
  1.4 3.0 %collective-permute-start = (bf16[1,4,2,256,256]{4,3,1,2,0:T(8,128)(2,1)S(1)}, bf16[1,4,2,256,256]{4,3,1,2,0:T(8,128)(2,1)S(1)}, u32[]{:S(2)}, u32[]{:S(2)}) collective-permute-start(bf16[1,4,2,256,256]{4,3,1,2,0:T(8,128)(2,1)S(1)} %copy.101), channel_id=1, source_target_pairs={{1,0},{2,1},{3,2},{4,3},{5,4},{6,5},{7,6},{8,7},{9,8},{10,9},{11,1... | collective-permute-start | bytes 3145736 | tf_op jit(solution)/shard_map/ppermute | solution.py:12
  4.5 0.3 fusion.19
  4.8 0.3 fusion.20
  5.1 0.3 fusion.9
  5.4 0.3 fusion.26
  5.7 0.6 copy-done.1
  6.4 0.3 fusion.10
  6.7 0.3 fusion.8
  7.0 0.3 fusion.25
  7.4 0.3 fusion.7
  7.7 21.7 %collective-permute-done = bf16[1,4,2,256,256]{4,3,1,2,0:T(8,128)(2,1)S(1)} collective-permute-done((bf16[1,4,2,256,256]{4,3,1,2,0:T(8,128)(2,1)S(1)}, bf16[1,4,2,256,256]{4,3,1,2,0:T(8,128)(2,1)S(1)}, u32[]{:S(2)}, u32[]{:S(2)}) %collective-permute-start) | collective-permute-done | bytes 1048608 | tf_op jit(solution)/shard_map/ppermute | solution.py:12
  29.4 0.3 fusion.22
  29.7 0.3 fusion.21
  30.0 0.3 fusion.11
  30.4 0.3 fusion.28
  30.7 0.3 fusion.12
  31.0 0.3 fusion.27
  31.3 0.3 fusion.6
  31.7 0.3 fusion.5
  32.0 0.4 fusion.3
  32.5 0.8 copy.65
  33.3 42.2 %all_to_all.36 = bf16[4,2,256,256]{3,0,1,2:T(4,128)(2,1)S(1)} all-to-all(bf16[4,2,256,256]{3,0,1,2:T(4,128)(2,1)S(1)} %copy.65), channel_id=1, replica_groups=mesh['energy'=32,'cuts'=16] {'energy'}, dimensions={2} | all-to-all | bytes 2097152 | tf_op jit(solution)/shard_map/all_to_all | solution.py:79
  75.5 0.2 copy.98
  75.7 0.1 copy.67
  75.9 0.1 copy.85
  76.1 0.1 copy.86
  76.3 1.1 fusion.55
  77.4 1.1 fusion.52
  78.5 1.1 convolution_add_fusion.1
  79.7 1.1 convolution_add_fusion
  80.8 0.9 fusion.1
  81.7 0.8 convolution_multiply_fusion.1
  82.5 0.8 convolution_multiply_fusion
  83.3 0.3 copy.87
  83.6 0.3 copy.88
  84.0 1.2 fusion.4
  85.1 4.9 %all-to-all-start.1 = ((bf16[128,2,8,256]{3,2,1,0:T(8,128)(2,1)}), bf16[128,2,8,256]{3,2,1,0:T(8,128)(2,1)S(1)}, u32[]{:S(2)}, u32[]{:S(2)}) async-start(bf16[128,2,8,256]{3,2,1,0:T(8,128)(2,1)} %fusion.4), calls=%async_computation.1 | async-start | bytes 2097152 | tf_op jit(solution)/shard_map/all_to_all | solution.py:81
  90.2 28.7 %all-to-all-done.1 = bf16[128,2,8,256]{3,2,1,0:T(8,128)(2,1)S(1)} async-done(((bf16[128,2,8,256]{3,2,1,0:T(8,128)(2,1)}), bf16[128,2,8,256]{3,2,1,0:T(8,128)(2,1)S(1)}, u32[]{:S(2)}, u32[]{:S(2)}) %all-to-all-start.1) | async-done | bytes 1048608 | tf_op jit(solution)/shard_map/all_to_all | solution.py:81
  118.9 0.4 fusion.23
  119.3 0.3 fusion.24
  119.6 0.3 fusion.13
  120.0 0.3 fusion.30
  120.3 0.4 fusion.14
  120.7 0.3 fusion.29
  121.0 0.3 fusion.18
  121.4 0.3 fusion.17
  121.9 1.0 copy.78
  (13 shorter events, 0.5 us)
Async XLA Ops:
  0.0 4.4 %copy-start = (bf16[1,4,2,256,256]{4,3,2,1,0:T(8,128)(2,1)S(1)}, bf16[1,4,2,256,256]{4,3,2,1,0:T(8,128)(2,1)}, u32[]{:S(2)}) copy-start(bf16[1,4,2,256,256]{4,3,2,1,0:T(8,128)(2,1)} %param.4) | copy-start | bytes 3145732
  1.4 28.0 %collective-permute-start = (bf16[1,4,2,256,256]{4,3,1,2,0:T(8,128)(2,1)S(1)}, bf16[1,4,2,256,256]{4,3,1,2,0:T(8,128)(2,1)S(1)}, u32[]{:S(2)}, u32[]{:S(2)}) collective-permute-start(bf16[1,4,2,256,256]{4,3,1,2,0:T(8,128)(2,1)S(1)} %copy.101), channel_id=1, source_target_pairs={{1,0},{2,1},{3,2},{4,3},{5,4},{6,5},{7,6},{8,7},{9,8},{10,9},{11,1... | collective-permute-start | bytes 3145736 | tf_op jit(solution)/shard_map/ppermute | solution.py:12
  5.1 1.2 copy-start.1
  84.0 6.1 %copy-start.2 = (bf16[1,4,2,256,256]{4,3,2,1,0:T(8,128)(2,1)S(1)}, bf16[1,4,2,256,256]{4,3,2,1,0:T(8,128)(2,1)}, u32[]{:S(2)}) copy-start(bf16[1,4,2,256,256]{4,3,2,1,0:T(8,128)(2,1)} %param.7) | copy-start | bytes 3145732
  85.1 33.7 %all-to-all-start.1 = ((bf16[128,2,8,256]{3,2,1,0:T(8,128)(2,1)}), bf16[128,2,8,256]{3,2,1,0:T(8,128)(2,1)S(1)}, u32[]{:S(2)}, u32[]{:S(2)}) async-start(bf16[128,2,8,256]{3,2,1,0:T(8,128)(2,1)} %fusion.4), calls=%async_computation.1 | async-start | bytes 2097152 | tf_op jit(solution)/shard_map/all_to_all | solution.py:81
where the time goes:
time: 123 us
  waiting for transfers between devices  50.4 us (41%)
  blocking collectives  42.2 us (34%)
  matrix products  13.9 us (11%)
  starting transfers between devices  7.91 us (6%)
  local copies, waits for them, and re-layouts  5.47 us (4%)
  other arithmetic  2.62 us (2%)
    all_to_all x1, blocking collectives, shards(): lax.all_to_all(lesser, 'energy', split_axis=2, concat_axis=0, tiled=True)  42.2 us
    all_to_all x1, waiting for transfers between devices, shards(): lax.all_to_all(polar_rows, 'energy', split_axis=0, concat_axis=2, tiled=T...  28.7 us
    ppermute x1, waiting for transfers between devices, shifted(): lax.ppermute(value, axis, [(source, source + steps) for source in range(l...  21.7 us
    all_to_all x1, starting transfers between devices, shards(): lax.all_to_all(polar_rows, 'energy', split_axis=0, concat_axis=2, tiled=T...  4.93 us
    unnamed x15, local copies, waits for them, and re-layouts  3.11 us
    ppermute x1, starting transfers between devices, shifted(): lax.ppermute(value, axis, [(source, source + steps) for source in range(l...  2.98 us
  transfers between devices with their start and end apart: 2, of which 2 were waited for; matrix products, arithmetic and copies ran while one was open for 2% of the time, Pallas kernels for 0%

commit v1 on v0

v1 whole, which is shorter than its diff:
```python
import functools
import math

import jax
import jax.numpy as jnp
import numpy as np
from jax import lax
from jax.experimental import pallas as pl
from jax.experimental.pallas import tpu as pltpu
from jax.sharding import PartitionSpec as P


F32 = jnp.float32
BF16 = jnp.bfloat16
FIRST = 1


def shifted(value, axis, steps):
    count = lax.axis_size(axis)
    leading, last = (max(0, -steps), min(count, count - steps))
    return lax.ppermute(value, axis, [(source, source + steps) for source in range(leading, last)])


def product(left, right):
    rows = left.shape[0] // 2
    by_real = jnp.dot(left, right[0], preferred_element_type=F32)
    by_imag = jnp.dot(left, right[1], preferred_element_type=F32)
    return by_real[:rows] - by_imag[rows:], by_real[rows:] + by_imag[:rows]


def product_adjoint(left, right):
    rows = left.shape[0] // 2
    turned = functools.partial(
        lax.dot_general, dimension_numbers=(((1,), (1,)), ((), ())), preferred_element_type=F32
    )
    by_real = turned(left, right[0])
    by_imag = turned(left, right[1])
    return by_real[:rows] + by_imag[rows:], by_real[rows:] - by_imag[:rows]


def stacked(ref):
    return ref[0, 0].reshape(-1, ref.shape[-1])


def joined(pair):
    return jnp.concatenate([part.astype(BF16) for part in pair], axis=0)


def own_kernel(green, sigma, out):
    term = joined(product(stacked(green), (sigma[0, 0, 0], sigma[0, 0, 1])))
    real, imag = product_adjoint(term, (green[0, 0, 0], green[0, 0, 1]))
    out[0, 0] = real
    out[0, 1] = imag


def pair_kernel(own, green, sigma, out):
    term = joined(product(stacked(green), (sigma[0, 0, 0], sigma[0, 0, 1])))
    real, imag = product_adjoint(term, (green[0, 0, 0], green[0, 0, 1]))
    shape = out.shape[0], out.shape[3], out.shape[4]
    out[:, 0, 0] = (real + own[0, 0]).astype(BF16).reshape(shape)
    out[:, 0, 1] = (imag + own[0, 1]).astype(BF16).reshape(shape)


def final_kernel(screening, polar, out):
    size = out.shape[-1]
    parts = tuple(polar[:, 0, part].reshape(size, size) for part in range(2))
    left = joined(product(stacked(screening), parts))
    real, imag = product_adjoint(left, (screening[0, 0, 0], screening[0, 0, 1]))
    out[0, 0, 0] = real.astype(BF16)
    out[0, 0, 1] = imag.astype(BF16)


def correlate_kernel(forward, inverse_even, inverse_odd, early, late, out):
    count = out.shape[1]

    def spectrum(part):
        data = jnp.concatenate([early[part], late[part]], axis=0)
        return jnp.dot(forward[...], jnp.concatenate([data, data], axis=0), preferred_element_type=F32)

    real, imag = spectrum(0), spectrum(1)
    even_real, odd_real = real[:count], real[count:]
    even_imag, odd_imag = imag[:count], imag[count:]
    even = even_real * even_real + even_imag * even_imag
    odd = odd_real * odd_real + odd_imag * odd_imag
    cross = (even_real * odd_imag - even_imag * odd_real).astype(BF16)
    power = jnp.concatenate([even.astype(BF16), odd.astype(BF16)], axis=0)
    out[0] = jnp.dot(inverse_even[...], power, preferred_element_type=F32).astype(BF16)
    out[1] = jnp.dot(
        inverse_odd[...], jnp.concatenate([cross, cross], axis=0), preferred_element_type=F32
    ).astype(BF16)


def split_table(table):
    upper = table.astype(jnp.bfloat16)
    lower = (table - upper.astype(np.float64)).astype(jnp.bfloat16)
    return np.concatenate([upper, lower], axis=1)


def tables(energies, order):
    period = 2 * energies
    index = np.arange(energies)
    angle = 2.0 * math.pi / period * (np.outer(index, order) % period)
    even, odd = np.cos(angle), np.sin(angle)
    odd[0] = np.where(order % 2 == 0, 1.0, -1.0)
    forward = split_table(np.concatenate([even, odd], axis=0))
    angle = 2.0 * math.pi / period * (np.outer(index, index) % period)
    scale = 1.0 / (period * energies)
    cos_inv, sin_inv = 2.0 * scale * np.cos(angle), np.sin(angle)
    cos_inv[:, 0] = scale
    nyquist = cos_inv.copy()
    nyquist[:, 0] = scale * np.where(index % 2 == 0, 1.0, -1.0)
    inverse_even = np.concatenate([cos_inv, nyquist], axis=1).astype(jnp.bfloat16)
    inverse_odd = split_table(4.0 * scale * sin_inv)
    return forward, inverse_even, inverse_odd


def params(**more):
    return pltpu.CompilerParams(vmem_limit_bytes=20 * 2**20, **more)


def cost(flops, accessed):
    return pl.CostEstimate(flops=flops, bytes_accessed=accessed, transcendentals=0)


def block_spec(size, start=0):
    return pl.BlockSpec((1, 1, 2, size, size), lambda j: (0, j + start, 0, 0, 0))


def shards(green_diag, green_upper, sigma_lesser, screening):
    local, size = green_diag.shape[1], green_diag.shape[-1]
    devices = lax.axis_size("energy")
    energies = local * devices
    group = size // devices
    unit = 16 * size**3
    plane = 2 * size * size
    cuts = (0, FIRST, local)
    sigma_next = []
    for start, stop in zip(cuts, cuts[1:]):
        sigma_next.append(shifted(sigma_lesser[:, start:stop], "cuts", -1))
    own = pl.pallas_call(
        own_kernel,
        grid=(local,),
        in_specs=[block_spec(size), block_spec(size)],
        out_specs=pl.BlockSpec((1, 2, size, size), lambda j: (j, 0, 0, 0)),
        out_shape=jax.ShapeDtypeStruct((local, 2, size, size), F32),
        compiler_params=params(),
        cost_estimate=cost(local * unit, local * plane * 8),
        name="own",
    )(green_diag, sigma_lesser)

    pieces = []
    for index, (start, stop) in enumerate(zip(cuts, cuts[1:])):
        count = stop - start
        lesser = pl.pallas_call(
            pair_kernel,
            grid=(count,),
            in_specs=[
                pl.BlockSpec((1, 2, size, size), lambda j, start=start: (j + start, 0, 0, 0)),
                block_spec(size, start),
                block_spec(size),
            ],
            out_specs=pl.BlockSpec((devices, 1, 2, group, size), lambda j: (0, j, 0, 0, 0)),
            out_shape=jax.ShapeDtypeStruct((devices, count, 2, group, size), BF16),
            compiler_params=params(),
            cost_estimate=cost(count * unit, count * plane * 10),
        )(own, green_upper, sigma_next[index])
        piece = lax.all_to_all(lesser, "energy", split_axis=0, concat_axis=0, tiled=True)
        pieces.append(
            piece.transpose(2, 0, 1, 3, 4).reshape(2, devices * count, group * size)
        )

    grid = np.arange(energies).reshape(devices, local)
    order = np.concatenate([grid[:, a:b].reshape(-1) for a, b in zip(cuts, cuts[1:])])
    constants = [jnp.asarray(table) for table in tables(energies, order)]
    width = group * size
    step = width // 4
    polar = pl.pallas_call(
        correlate_kernel,
        grid=(width // step,),
        in_specs=[pl.BlockSpec(table.shape, lambda i: (0, 0)) for table in constants]
        + [pl.BlockSpec((2, piece.shape[1], step), lambda i: (0, 0, i)) for piece in pieces],
        out_specs=pl.BlockSpec((2, energies, step), lambda i: (0, 0, i)),
        out_shape=jax.ShapeDtypeStruct((2, energies, width), BF16),
        compiler_params=params(),
        cost_estimate=cost(2 * 2 * 256 * 256 * width * 2, energies * width * 8),
        name="correlate",
    )(*constants, *pieces)
    rows = polar.transpose(1, 0, 2).reshape(devices, local, 2, group, size)
    field = lax.all_to_all(rows, "energy", split_axis=0, concat_axis=0, tiled=True)

    return pl.pallas_call(
        final_kernel,
        grid=(local,),
        in_specs=[
            block_spec(size),
            pl.BlockSpec((devices, 1, 2, group, size), lambda j: (0, j, 0, 0, 0)),
        ],
        out_specs=block_spec(size),
        out_shape=jax.ShapeDtypeStruct(screening.shape, BF16),
        compiler_params=params(),
        cost_estimate=cost(local * unit, local * plane * 6),
        name="final",
    )(screening, field)


def solution(mesh):
    spec = P("cuts", "energy", None, None, None)
    return jax.shard_map(
        shards, mesh=mesh, in_specs=(spec, spec, spec, spec), out_specs=spec, check_vma=False
    )
```

time: 123 us -> 127 us (1.033)
  starting transfers between devices: 7.91 us -> 24.6 us
  Pallas kernels: 0 us -> 14 us
  matrix products: 13.9 us -> 0 us
  blocking collectives: 42.2 us -> 33.8 us
  other arithmetic: 2.62 us -> 0 us
  waiting for transfers between devices: 50.4 us -> 48.8 us
    pallas_call x0 -> x5, Pallas kernels: none -> 14 us  [the longest x2 4.89 us: shards(): pl.pallas_call(pair_kernel, grid=(count,), in_specs=[pl.BlockSpec((1, 2,...]
    dot_general x30 -> x0, matrix products: 13.9 us -> none  [the longest x2 2.26 us: split_table_dot(): jnp.dot(lower, data, preferred_element_type=jnp.float32)]
    all_to_all x1 -> x2, starting transfers between devices: 4.93 us -> 18.5 us  [shards(): lax.all_to_all(lesser, 'energy', split_axis=0, concat_axis=0, tiled=True)]
    all_to_all x1, blocking collectives: 42.2 us -> 33.8 us  [shards(): lax.all_to_all(rows, 'energy', split_axis=0, concat_axis=0, tiled=True)]
    ppermute x1 -> x2, waiting for transfers between devices: 21.7 us -> 18.1 us  [shifted(): lax.ppermute(value, axis, [(source, source + steps) for source in range(l...]
    slice x1 -> x2, local copies, waits for them, and re-layouts: 0.07 us -> 3.18 us  [shards(): sigma_next.append(shifted(sigma_lesser[:, start:stop], 'cuts', -1))]
    ppermute x1 -> x2, starting transfers between devices: 2.98 us -> 6.07 us  [shifted(): lax.ppermute(value, axis, [(source, source + steps) for source in range(l...]
    all_to_all x1 -> x2, waiting for transfers between devices: 28.7 us -> 30.7 us  [shards(): lax.all_to_all(lesser, 'energy', split_axis=0, concat_axis=0, tiled=True)]
  transfers between devices with their start and end apart: 2 -> 4, of which waited for: 2 -> 3; matrix products, arithmetic and copies ran while one was open for 2% -> 1% of each run, Pallas kernels for 0% -> 6%
where the time goes in v1:
time: 127 us
  waiting for transfers between devices  48.8 us (38%)
  blocking collectives  33.8 us (27%)
  starting transfers between devices  24.6 us (19%)
  Pallas kernels  14 us (11%)
  local copies, waits for them, and re-layouts  5.05 us (4%)
    all_to_all x1, blocking collectives, shards(): lax.all_to_all(rows, 'energy', split_axis=0, concat_axis=0, tiled=True)  33.8 us
    all_to_all x2, waiting for transfers between devices, shards(): lax.all_to_all(lesser, 'energy', split_axis=0, concat_axis=0, tiled=True)  30.7 us
    all_to_all x2, starting transfers between devices, shards(): lax.all_to_all(lesser, 'energy', split_axis=0, concat_axis=0, tiled=True)  18.5 us
    ppermute x2, waiting for transfers between devices, shifted(): lax.ppermute(value, axis, [(source, source + steps) for source in range(l...  18.1 us
    ppermute x2, starting transfers between devices, shifted(): lax.ppermute(value, axis, [(source, source + steps) for source in range(l...  6.07 us
    pallas_call x2, Pallas kernels, shards(): pl.pallas_call(pair_kernel, grid=(count,), in_specs=[pl.BlockSpec((1, 2,...  4.89 us
    pallas_call x1, Pallas kernels, shards(): pl.pallas_call(final_kernel, grid=(local,), in_specs=[block_spec(size), p...  3.81 us
    slice x2, local copies, waits for them, and re-layouts, shards(): sigma_next.append(shifted(sigma_lesser[:, start:stop], 'cuts', -1))  3.18 us
  transfers between devices with their start and end apart: 4, of which 3 were waited for; matrix products, arithmetic and copies ran while one was open for 1% of the time, Pallas kernels for 6%

profile of v1, /device:TPU:57, one launch (start us, length us, event | category | flops | bytes accessed | tf_op | source)
XLA Modules:
  0.0 126.6 jit_solution(4103213473656235194)
XLA Ops:
  0.0 0.0 copy-start.1
  0.0 0.0 copy-start.3
  0.0 2.2 %slice.7 = bf16[1,3,2,256,256]{4,3,2,1,0:T(8,128)(2,1)} slice(bf16[1,4,2,256,256]{4,3,2,1,0:T(8,128)(2,1)} %sigma.1), slice={[0:1], [1:4], [0:2], [0:256], [0:256]} | slice | bytes 1572864 | tf_op jit(solution)/shard_map/slice | solution.py:139
  2.2 3.0 %collective-permute-start.1 = (bf16[1,3,2,256,256]{4,3,2,1,0:T(8,128)(2,1)}, bf16[1,3,2,256,256]{4,3,2,1,0:T(8,128)(2,1)}, u32[]{:S(2)}, u32[]{:S(2)}) collective-permute-start(bf16[1,3,2,256,256]{4,3,2,1,0:T(8,128)(2,1)} %slice.7), channel_id=1, source_target_pairs={{1,0},{2,1},{3,2},{4,3},{5,4},{6,5},{7,6},{8,7},{9,8},{10,9},{11,1... | collective-permute-start | bytes 2359304 | tf_op jit(solution)/shard_map/ppermute | solution.py:21
  5.2 1.0 slice.6
  6.2 0.0 copy-start
  6.2 3.1 %collective-permute-start = (bf16[1,1,2,256,256]{4,3,2,1,0:T(8,128)(2,1)S(1)}, bf16[1,1,2,256,256]{4,3,2,1,0:T(8,128)(2,1)S(1)}, u32[]{:S(2)}, u32[]{:S(2)}) collective-permute-start(bf16[1,1,2,256,256]{4,3,2,1,0:T(8,128)(2,1)S(1)} %slice.6), channel_id=1, source_target_pairs={{1,0},{2,1},{3,2},{4,3},{5,4},{6,5},{7,6},{8,7},{9,8},{10,9},{11,1... | collective-permute-start | bytes 786440 | tf_op jit(solution)/shard_map/ppermute | solution.py:21
  9.3 0.0 copy-done.1
  9.3 0.0 copy-done.3
  9.3 3.0 %own.1 = f32[4,2,256,256]{3,2,1,0:T(8,128)S(1)} custom-call(bf16[1,4,2,256,256]{4,3,2,1,0:T(8,128)(2,1)S(1)} %copy-done.3, bf16[1,4,2,256,256]{4,3,2,1,0:T(8,128)(2,1)S(1)} %copy-done.1), custom_call_target="tpu_custom_call" | custom-call | flops 1073741824 | bytes 4194304 | tf_op jit(solution)/shard_map/own/pallas_call | solution.py:140
  12.3 18.1 %collective-permute-done.sigma = bf16[1,1,2,256,256]{4,3,2,1,0:T(8,128)(2,1)S(1)} collective-permute-done((bf16[1,1,2,256,256]{4,3,2,1,0:T(8,128)(2,1)S(1)}, bf16[1,1,2,256,256]{4,3,2,1,0:T(8,128)(2,1)S(1)}, u32[]{:S(2)}, u32[]{:S(2)}) %collective-permute-start) | collective-permute-done | bytes 262176 | tf_op jit(solution)/shard_map/ppermute | solution.py:21
  30.5 0.0 copy-done
  30.5 1.5 %shard_map.73 = bf16[32,1,2,8,256]{4,3,2,1,0:T(8,128)(2,1)} custom-call(f32[4,2,256,256]{3,2,1,0:T(8,128)S(1)} %own.1, bf16[1,4,2,256,256]{4,3,2,1,0:T(8,128)(2,1)S(1)} %copy-done, bf16[1,1,2,256,256]{4,3,2,1,0:T(8,128)(2,1)S(1)} %collective-permute-done.sigma), custom_call_target="tpu_custom_call" | custom-call | flops 268435456 | bytes 1310720 | tf_op jit(solution)/shard_map/pallas_call | solution.py:154
  31.9 14.5 %all-to-all-start = ((bf16[32,1,2,8,256]{4,3,2,1,0:T(8,128)(2,1)}), bf16[32,1,2,8,256]{4,3,2,1,0:T(8,128)(2,1)S(1)}, u32[]{:S(2)}, u32[]{:S(2)}) async-start(bf16[32,1,2,8,256]{4,3,2,1,0:T(8,128)(2,1)} %shard_map.73), calls=%async_computation | async-start | bytes 524288 | tf_op jit(solution)/shard_map/all_to_all | solution.py:167
  46.4 0.0 collective-permute-done.1.sigma
  46.4 3.4 %shard_map.74 = bf16[32,3,2,8,256]{4,3,2,1,0:T(8,128)(2,1)S(1)} custom-call(f32[4,2,256,256]{3,2,1,0:T(8,128)S(1)} %own.1, bf16[1,4,2,256,256]{4,3,2,1,0:T(8,128)(2,1)S(1)} %copy-done, bf16[1,3,2,256,256]{4,3,2,1,0:T(8,128)(2,1)} %collective-permute-done.1.sigma), custom_call_target="tpu_custom_call" | custom-call | flops 805306368 | bytes 3932160 | tf_op jit(solution)/shard_map/pallas_call | solution.py:154
  49.8 0.0 copy-start.2
  49.8 0.9 copy-done.2
  50.7 8.3 %all-to-all-done = bf16[32,1,2,8,256]{4,3,2,1,0:T(8,128)(2,1)S(1)} async-done(((bf16[32,1,2,8,256]{4,3,2,1,0:T(8,128)(2,1)}), bf16[32,1,2,8,256]{4,3,2,1,0:T(8,128)(2,1)S(1)}, u32[]{:S(2)}, u32[]{:S(2)}) %all-to-all-start) | async-done | bytes 262176 | tf_op jit(solution)/shard_map/all_to_all | solution.py:167
  59.0 4.1 %all-to-all-start.1 = ((bf16[32,3,2,8,256]{4,3,2,1,0:T(8,128)(2,1)}), bf16[32,3,2,8,256]{4,3,2,1,0:T(8,128)(2,1)S(1)}, u32[]{:S(2)}, u32[]{:S(2)}) async-start(bf16[32,3,2,8,256]{4,3,2,1,0:T(8,128)(2,1)} %copy-done.2), calls=%async_computation.1 | async-start | bytes 1572864 | tf_op jit(solution)/shard_map/all_to_all | solution.py:167
  63.1 0.0 copy-start.5
  63.1 0.0 copy-start.6
  63.1 0.0 copy-start.7
  63.1 0.1 reshape.12
  63.2 0.1 copy.11.early
  63.3 22.4 %all-to-all-done.1 = bf16[32,3,2,8,256]{4,3,2,1,0:T(8,128)(2,1)S(1)} async-done(((bf16[32,3,2,8,256]{4,3,2,1,0:T(8,128)(2,1)}), bf16[32,3,2,8,256]{4,3,2,1,0:T(8,128)(2,1)S(1)}, u32[]{:S(2)}, u32[]{:S(2)}) %all-to-all-start.1) | async-done | bytes 786464 | tf_op jit(solution)/shard_map/all_to_all | solution.py:167
  85.7 0.2 reshape.13
  85.9 0.2 copy.12.late
  86.2 0.0 copy-done.5
  86.2 0.0 copy-done.6
  86.2 0.0 copy-done.7
  86.2 2.3 %correlate.1 = bf16[2,128,2048]{2,1,0:T(8,128)(2,1)S(1)} custom-call(bf16[256,256]{1,0:T(8,128)(2,1)S(1)} %copy-done.5, bf16[128,256]{1,0:T(8,128)(2,1)S(1)} %copy-done.6, bf16[128,256]{1,0:T(8,128)(2,1)S(1)} %copy-done.7, bf16[2,32,2048]{2,1,0:T(8,128)(2,1)S(1)} %copy.11.early, bf16[2,96,2048]{2,1,0:T(8,128)(2,1)S(1)} %copy.12.late), custom_call_target="tpu_custom_call" | custom-call | flops 1073741824 | bytes 2097152 | tf_op jit(solution)/shard_map/correlate/pallas_call | solution.py:177
  88.5 0.3 copy.14
  88.8 0.0 copy-start.4
  88.8 0.1 copy.13
  88.9 33.8 %all_to_all.15.polar = bf16[32,4,2,8,256]{4,3,2,1,0:T(8,128)(2,1)S(1)} all-to-all(bf16[32,4,2,8,256]{4,3,2,1,0:T(8,128)(2,1)S(1)} %copy.13), channel_id=1, replica_groups=mesh['energy'=32,'cuts'=16] {'energy'}, dimensions={0} | all-to-all | bytes 2097152 | tf_op jit(solution)/shard_map/all_to_all | solution.py:189
  122.7 0.0 copy-done.4
  122.7 3.8 %final.1 = bf16[1,4,2,256,256]{4,3,2,1,0:T(8,128)(2,1)} custom-call(bf16[1,4,2,256,256]{4,3,2,1,0:T(8,128)(2,1)S(1)} %copy-done.4, bf16[32,4,2,8,256]{4,3,2,1,0:T(8,128)(2,1)S(1)} %all_to_all.15.polar), custom_call_target="tpu_custom_call" | custom-call | flops 1073741824 | bytes 3145728 | tf_op jit(solution)/shard_map/final/pallas_call | solution.py:191
Async XLA Ops:
  0.0 9.3 %copy-start.1 = (bf16[1,4,2,256,256]{4,3,2,1,0:T(8,128)(2,1)S(1)}, bf16[1,4,2,256,256]{4,3,2,1,0:T(8,128)(2,1)}, u32[]{:S(2)}) copy-start(bf16[1,4,2,256,256]{4,3,2,1,0:T(8,128)(2,1)} %sigma.1) | copy-start | bytes 3145732
  0.0 9.3 %copy-start.3 = (bf16[1,4,2,256,256]{4,3,2,1,0:T(8,128)(2,1)S(1)}, bf16[1,4,2,256,256]{4,3,2,1,0:T(8,128)(2,1)}, u32[]{:S(2)}) copy-start(bf16[1,4,2,256,256]{4,3,2,1,0:T(8,128)(2,1)} %green.3) | copy-start | bytes 3145732
  2.2 44.2 %collective-permute-start.1 = (bf16[1,3,2,256,256]{4,3,2,1,0:T(8,128)(2,1)}, bf16[1,3,2,256,256]{4,3,2,1,0:T(8,128)(2,1)}, u32[]{:S(2)}, u32[]{:S(2)}) collective-permute-start(bf16[1,3,2,256,256]{4,3,2,1,0:T(8,128)(2,1)} %slice.7), channel_id=1, source_target_pairs={{1,0},{2,1},{3,2},{4,3},{5,4},{6,5},{7,6},{8,7},{9,8},{10,9},{11,1... | collective-permute-start | bytes 2359304 | tf_op jit(solution)/shard_map/ppermute | solution.py:21
  6.2 24.3 %copy-start = (bf16[1,4,2,256,256]{4,3,2,1,0:T(8,128)(2,1)S(1)}, bf16[1,4,2,256,256]{4,3,2,1,0:T(8,128)(2,1)}, u32[]{:S(2)}) copy-start(bf16[1,4,2,256,256]{4,3,2,1,0:T(8,128)(2,1)} %green.5) | copy-start | bytes 3145732
  6.2 24.3 %collective-permute-start = (bf16[1,1,2,256,256]{4,3,2,1,0:T(8,128)(2,1)S(1)}, bf16[1,1,2,256,256]{4,3,2,1,0:T(8,128)(2,1)S(1)}, u32[]{:S(2)}, u32[]{:S(2)}) collective-permute-start(bf16[1,1,2,256,256]{4,3,2,1,0:T(8,128)(2,1)S(1)} %slice.6), channel_id=1, source_target_pairs={{1,0},{2,1},{3,2},{4,3},{5,4},{6,5},{7,6},{8,7},{9,8},{10,9},{11,1... | collective-permute-start | bytes 786440 | tf_op jit(solution)/shard_map/ppermute | solution.py:21
  31.9 27.1 %all-to-all-start = ((bf16[32,1,2,8,256]{4,3,2,1,0:T(8,128)(2,1)}), bf16[32,1,2,8,256]{4,3,2,1,0:T(8,128)(2,1)S(1)}, u32[]{:S(2)}, u32[]{:S(2)}) async-start(bf16[32,1,2,8,256]{4,3,2,1,0:T(8,128)(2,1)} %shard_map.73), calls=%async_computation | async-start | bytes 524288 | tf_op jit(solution)/shard_map/all_to_all | solution.py:167
  49.8 0.9 copy-start.2
  59.0 26.7 %all-to-all-start.1 = ((bf16[32,3,2,8,256]{4,3,2,1,0:T(8,128)(2,1)}), bf16[32,3,2,8,256]{4,3,2,1,0:T(8,128)(2,1)S(1)}, u32[]{:S(2)}, u32[]{:S(2)}) async-start(bf16[32,3,2,8,256]{4,3,2,1,0:T(8,128)(2,1)} %copy-done.2), calls=%async_computation.1 | async-start | bytes 1572864 | tf_op jit(solution)/shard_map/all_to_all | solution.py:167
  63.1 23.1 %copy-start.5 = (bf16[256,256]{1,0:T(8,128)(2,1)S(1)}, bf16[256,256]{1,0:T(8,128)(2,1)}, u32[]{:S(2)}) copy-start(bf16[256,256]{1,0:T(8,128)(2,1)} %constant.6.clone.forward) | copy-start | bytes 393220
  63.1 23.0 %copy-start.6 = (bf16[128,256]{1,0:T(8,128)(2,1)S(1)}, bf16[128,256]{1,0:T(8,128)(2,1)}, u32[]{:S(2)}) copy-start(bf16[128,256]{1,0:T(8,128)(2,1)} %constant.7.clone.inverse_even) | copy-start | bytes 196612
  63.1 23.0 %copy-start.7 = (bf16[128,256]{1,0:T(8,128)(2,1)S(1)}, bf16[128,256]{1,0:T(8,128)(2,1)}, u32[]{:S(2)}) copy-start(bf16[128,256]{1,0:T(8,128)(2,1)} %constant.8.clone.inverse_odd) | copy-start | bytes 196612
  88.8 33.9 %copy-start.4 = (bf16[1,4,2,256,256]{4,3,2,1,0:T(8,128)(2,1)S(1)}, bf16[1,4,2,256,256]{4,3,2,1,0:T(8,128)(2,1)}, u32[]{:S(2)}) copy-start(bf16[1,4,2,256,256]{4,3,2,1,0:T(8,128)(2,1)} %screening.1) | copy-start | bytes 3145732

commit v2 on v1

--- a/solution.py
+++ b/solution.py
@@ -12,7 +12,7 @@
 
 F32 = jnp.float32
 BF16 = jnp.bfloat16
-FIRST = 1
+CHUNK = 2
 
 
 def shifted(value, axis, steps):
@@ -38,36 +38,61 @@
     return by_real[:rows] + by_imag[rows:], by_real[rows:] - by_imag[:rows]
 
 
-def stacked(ref):
-    return ref[0, 0].reshape(-1, ref.shape[-1])
+def pair_of(ref, j):
+    return ref[0, j, 0], ref[0, j, 1]
 
 
 def joined(pair):
     return jnp.concatenate([part.astype(BF16) for part in pair], axis=0)
 
 
+def halves(ref, j):
+    rows = ref.shape[-2] // 2
+    return [
+        jnp.concatenate([ref[0, j, part, start : start + rows] for part in range(2)], axis=0)
+        for start in (0, rows)
+    ]
+
+
+def sandwich(outer, inner):
+    count = outer.shape[1]
+    terms = [
+        [joined(product(half, inner(j))) for half in halves(outer, j)] for j in range(count)
+    ]
+    return [[product_adjoint(term, pair_of(outer, j)) for term in terms[j]] for j in range(count)]
+
+
 def own_kernel(green, sigma, out):
-    term = joined(product(stacked(green), (sigma[0, 0, 0], sigma[0, 0, 1])))
-    real, imag = product_adjoint(term, (green[0, 0, 0], green[0, 0, 1]))
-    out[0, 0] = real
-    out[0, 1] = imag
+    rows = out.shape[-2] // 2
+    for j, sides in enumerate(sandwich(green, lambda j: pair_of(sigma, j))):
+        for side, parts in enumerate(sides):
+            for part in range(2):
+                out[j, part, side * rows : (side + 1) * rows] = parts[part]
 
 
 def pair_kernel(own, green, sigma, out):
-    term = joined(product(stacked(green), (sigma[0, 0, 0], sigma[0, 0, 1])))
-    real, imag = product_adjoint(term, (green[0, 0, 0], green[0, 0, 1]))
-    shape = out.shape[0], out.shape[3], out.shape[4]
-    out[:, 0, 0] = (real + own[0, 0]).astype(BF16).reshape(shape)
-    out[:, 0, 1] = (imag + own[0, 1]).astype(BF16).reshape(shape)
+    devices, group, size = out.shape[0], out.shape[3], out.shape[4]
+    rows, half = size // 2, devices // 2
+    for j, sides in enumerate(sandwich(green, lambda j: pair_of(sigma, j))):
+        for side, parts in enumerate(sides):
+            for part in range(2):
+                total = parts[part] + own[j, part, side * rows : (side + 1) * rows]
+                out[side * half : (side + 1) * half, j, part] = total.astype(BF16).reshape(
+                    half, group, size
+                )
 
 
 def final_kernel(screening, polar, out):
     size = out.shape[-1]
-    parts = tuple(polar[:, 0, part].reshape(size, size) for part in range(2))
-    left = joined(product(stacked(screening), parts))
-    real, imag = product_adjoint(left, (screening[0, 0, 0], screening[0, 0, 1]))
-    out[0, 0, 0] = real.astype(BF16)
-    out[0, 0, 1] = imag.astype(BF16)
+    rows = size // 2
+
+    def inner(j):
+        return tuple(polar[:, j, part].reshape(size, size) for part in range(2))
+
+    for j, sides in enumerate(sandwich(screening, inner)):
+        for side, parts in enumerate(sides):
+            for part in range(2):
+                out[0, j, part, side * rows : (side + 1) * rows] = parts[part].astype(BF16)
 
 
 def correlate_kernel(forward, inverse_even, inverse_odd, early, late, out):
@@ -114,16 +139,12 @@
     return forward, inverse_even, inverse_odd
 
 
-def params(**more):
-    return pltpu.CompilerParams(vmem_limit_bytes=20 * 2**20, **more)
+def params(mebibytes=20):
+    return pltpu.CompilerParams(vmem_limit_bytes=mebibytes * 2**20)
 
 
 def cost(flops, accessed):
     return pl.CostEstimate(flops=flops, bytes_accessed=accessed, transcendentals=0)
-
-
-def block_spec(size, start=0):
-    return pl.BlockSpec((1, 1, 2, size, size), lambda j: (0, j + start, 0, 0, 0))
 
 
 def shards(green_diag, green_upper, sigma_lesser, screening):
@@ -133,15 +154,27 @@
     group = size // devices
     unit = 16 * size**3
     plane = 2 * size * size
-    cuts = (0, FIRST, local)
+    chunks = local // CHUNK
+    blocks = (1, CHUNK, 2, size, size)
+
+    def each(j):
+        return (0, j, 0, 0, 0)
+
+    def own_spec(start):
+        return pl.BlockSpec((CHUNK, 2, size, size), lambda j: (j + start, 0, 0, 0))
+
+    def rows_spec(start=0):
+        return pl.BlockSpec((devices, CHUNK, 2, group, size), lambda j: (0, j + start, 0, 0, 0))
+
     sigma_next = []
-    for start, stop in zip(cuts, cuts[1:]):
-        sigma_next.append(shifted(sigma_lesser[:, start:stop], "cuts", -1))
+    for index in range(chunks):
+        part = sigma_lesser[:, index * CHUNK : (index + 1) * CHUNK]
+        sigma_next.append(shifted(part, "cuts", -1))
     own = pl.pallas_call(
         own_kernel,
-        grid=(local,),
-        in_specs=[block_spec(size), block_spec(size)],
-        out_specs=pl.BlockSpec((1, 2, size, size), lambda j: (j, 0, 0, 0)),
+        grid=(chunks,),
+        in_specs=[pl.BlockSpec(blocks, each)] * 2,
+        out_specs=own_spec(0),
         out_shape=jax.ShapeDtypeStruct((local, 2, size, size), F32),
         compiler_params=params(),
         cost_estimate=cost(local * unit, local * plane * 8),
@@ -149,31 +182,30 @@
     )(green_diag, sigma_lesser)
 
     pieces = []
-    for index, (start, stop) in enumerate(zip(cuts, cuts[1:])):
-        count = stop - start
+    for index in range(chunks):
         lesser = pl.pallas_call(
             pair_kernel,
-            grid=(count,),
+            grid=(1,),
             in_specs=[
-                pl.BlockSpec((1, 2, size, size), lambda j, start=start: (j + start, 0, 0, 0)),
-                block_spec(size, start),
-                block_spec(size),
+                own_spec(index),
+                pl.BlockSpec(blocks, lambda j, index=index: (0, j + index, 0, 0, 0)),
+                pl.BlockSpec(blocks, each),
             ],
-            out_specs=pl.BlockSpec((devices, 1, 2, group, size), lambda j: (0, j, 0, 0, 0)),
-            out_shape=jax.ShapeDtypeStruct((devices, count, 2, group, size), BF16),
+            out_specs=rows_spec(),
+            out_shape=pltpu.HBM((devices, CHUNK, 2, group, size), BF16),
             compiler_params=params(),
-            cost_estimate=cost(count * unit, count * plane * 10),
+            cost_estimate=cost(CHUNK * unit, CHUNK * plane * 10),
         )(own, green_upper, sigma_next[index])
         piece = lax.all_to_all(lesser, "energy", split_axis=0, concat_axis=0, tiled=True)
         pieces.append(
-            piece.transpose(2, 0, 1, 3, 4).reshape(2, devices * count, group * size)
+            piece.transpose(2, 0, 1, 3, 4).reshape(2, devices * CHUNK, group * size)
         )
 
-    grid = np.arange(energies).reshape(devices, local)
-    order = np.concatenate([grid[:, a:b].reshape(-1) for a, b in zip(cuts, cuts[1:])])
+    grid = np.arange(energies).reshape(devices, chunks, CHUNK)
+    order = grid.transpose(1, 0, 2).reshape(-1)
     constants = [jnp.asarray(table) for table in tables(energies, order)]
     width = group * size
-    step = width // 4
+    step = width // 2
     polar = pl.pallas_call(
         correlate_kernel,
         grid=(width // step,),
@@ -190,12 +222,9 @@
 
     return pl.pallas_call(
         final_kernel,
-        grid=(local,),
-        in_specs=[
-            block_spec(size),
-            pl.BlockSpec((devices, 1, 2, group, size), lambda j: (0, j, 0, 0, 0)),
-        ],
-        out_specs=block_spec(size),
+        grid=(chunks,),
+        in_specs=[pl.BlockSpec(blocks, each), rows_spec()],
+        out_specs=pl.BlockSpec(blocks, each),
         out_shape=jax.ShapeDtypeStruct(screening.shape, BF16),
         compiler_params=params(),
         cost_estimate=cost(local * unit, local * plane * 6),

time: 127 us -> 125 us (0.984)
  Pallas kernels: 14 us -> 8.53 us
  starting transfers between devices: 24.6 us -> 29.5 us
    all_to_all x2, waiting for transfers between devices: 30.7 us -> 16.6 us  [shards(): lax.all_to_all(lesser, 'energy', split_axis=0, concat_axis=0, tiled=True)]
    ppermute x2, waiting for transfers between devices: 18.1 us -> 31.1 us  [shifted(): lax.ppermute(value, axis, [(source, source + steps) for source in range(l...]
    all_to_all x2, starting transfers between devices: 18.5 us -> 24.5 us  [shards(): lax.all_to_all(lesser, 'energy', split_axis=0, concat_axis=0, tiled=True)]
    pallas_call x4, Pallas kernels: 11.7 us -> 6.8 us  [the longest x2 3.01 us: shards(): pl.pallas_call(pair_kernel, grid=(1,), in_specs=[own_spec(index), pl.Bloc...]
    slice x2 -> x1, local copies, waits for them, and re-layouts: 3.18 us -> 2.21 us  [shards(): part = sigma_lesser[:, index * CHUNK:(index + 1) * CHUNK]]
  transfers between devices with their start and end apart: 4 -> 4, of which waited for: 3 -> 3; matrix products, arithmetic and copies ran while one was open for 1% -> 1% of each run, Pallas kernels for 6% -> 2%
where the time goes in v2:
time: 125 us; the launch traced here: 124 us
  waiting for transfers between devices  47.7 us (38%)
  blocking collectives  34.1 us (27%)
  starting transfers between devices  29.5 us (24%)
  Pallas kernels  8.53 us (7%)
  local copies, waits for them, and re-layouts  4.28 us (3%)
    all_to_all x1, blocking collectives, shards(): lax.all_to_all(rows, 'energy', split_axis=0, concat_axis=0, tiled=True)  34.1 us
    ppermute x2, waiting for transfers between devices, shifted(): lax.ppermute(value, axis, [(source, source + steps) for source in range(l...  31.1 us
    all_to_all x2, starting transfers between devices, shards(): lax.all_to_all(lesser, 'energy', split_axis=0, concat_axis=0, tiled=True)  24.5 us
    all_to_all x2, waiting for transfers between devices, shards(): lax.all_to_all(lesser, 'energy', split_axis=0, concat_axis=0, tiled=True)  16.6 us
    ppermute x2, starting transfers between devices, shifted(): lax.ppermute(value, axis, [(source, source + steps) for source in range(l...  5.02 us
    pallas_call x2, Pallas kernels, shards(): pl.pallas_call(pair_kernel, grid=(1,), in_specs=[own_spec(index), pl.Bloc...  3.01 us
  transfers between devices with their start and end apart: 4, of which 3 were waited for; matrix products, arithmetic and copies ran while one was open for 1% of the time, Pallas kernels for 2%

profile of v2, /device:TPU:57, one launch (start us, length us, event | category | flops | bytes accessed | tf_op | source)
XLA Modules:
  0.0 124.3 jit_solution(10897882326542285886)
XLA Ops:
  0.0 0.0 copy-start
  0.0 0.0 copy-start.2
  0.0 2.2 %fusion = (bf16[1,2,2,256,256]{4,3,2,1,0:T(8,128)(2,1)}, bf16[1,2,2,256,256]{4,3,2,1,0:T(8,128)(2,1)S(1)}) fusion(bf16[1,4,2,256,256]{4,3,2,1,0:T(8,128)(2,1)} %sigma.1), kind=kLoop, calls=%fused_computation | loop fusion | bytes 2097152 | tf_op jit(solution)/shard_map/slice | solution.py:171
  2.2 0.0 copy-start.1
  2.2 3.1 %collective-permute-start = (bf16[1,2,2,256,256]{4,3,2,1,0:T(8,128)(2,1)S(1)}, bf16[1,2,2,256,256]{4,3,2,1,0:T(8,128)(2,1)S(1)}, u32[]{:S(2)}, u32[]{:S(2)}) collective-permute-start(bf16[1,2,2,256,256]{4,3,2,1,0:T(8,128)(2,1)S(1)} %get-tuple-element.6), channel_id=1, source_target_pairs={{1,0},{2,1},{3,2},{4,3},{5,4},{6,5},{7,6},{8,7},{9,8},{10,9},{11,1... | collective-permute-start | bytes 1572872 | tf_op jit(solution)/shard_map/ppermute | solution.py:21
  5.3 0.0 copy-done
  5.3 0.0 copy-done.2
  5.3 1.5 %own.1 = f32[4,2,256,256]{3,2,1,0:T(8,128)S(1)} custom-call(bf16[1,4,2,256,256]{4,3,2,1,0:T(8,128)(2,1)S(1)} %copy-done.2, bf16[1,4,2,256,256]{4,3,2,1,0:T(8,128)(2,1)S(1)} %copy-done), custom_call_target="tpu_custom_call" | custom-call | flops 1073741824 | bytes 4194304 | tf_op jit(solution)/shard_map/own/pallas_call | solution.py:173
  6.8 12.3 %collective-permute-done.sigma = bf16[1,2,2,256,256]{4,3,2,1,0:T(8,128)(2,1)S(1)} collective-permute-done((bf16[1,2,2,256,256]{4,3,2,1,0:T(8,128)(2,1)S(1)}, bf16[1,2,2,256,256]{4,3,2,1,0:T(8,128)(2,1)S(1)}, u32[]{:S(2)}, u32[]{:S(2)}) %collective-permute-start) | collective-permute-done | bytes 524320 | tf_op jit(solution)/shard_map/ppermute | solution.py:21
  19.1 0.0 copy-done.1
  19.1 1.5 %shard_map.73 = bf16[32,2,2,8,256]{4,3,2,1,0:T(8,128)(2,1)} custom-call(f32[4,2,256,256]{3,2,1,0:T(8,128)S(1)} %own.1, bf16[1,4,2,256,256]{4,3,2,1,0:T(8,128)(2,1)S(1)} %copy-done.1, bf16[1,2,2,256,256]{4,3,2,1,0:T(8,128)(2,1)S(1)} %collective-permute-done.sigma), custom_call_target="tpu_custom_call" | custom-call | flops 536870912 | bytes 2621440 | tf_op jit(solution)/shard_map/pallas_call | solution.py:186
  20.7 14.5 %all-to-all-start = ((bf16[32,2,2,8,256]{4,3,2,1,0:T(8,128)(2,1)}), bf16[32,2,2,8,256]{4,3,2,1,0:T(8,128)(2,1)}, u32[]{:S(2)}, u32[]{:S(2)}) async-start(bf16[32,2,2,8,256]{4,3,2,1,0:T(8,128)(2,1)} %shard_map.73), calls=%async_computation | async-start | bytes 1048576 | tf_op jit(solution)/shard_map/all_to_all | solution.py:199
  35.2 1.9 %collective-permute-start.1 = (bf16[1,2,2,256,256]{4,3,2,1,0:T(8,128)(2,1)}, bf16[1,2,2,256,256]{4,3,2,1,0:T(8,128)(2,1)S(1)}, u32[]{:S(2)}, u32[]{:S(2)}) collective-permute-start(bf16[1,2,2,256,256]{4,3,2,1,0:T(8,128)(2,1)} %get-tuple-element.5), channel_id=1, source_target_pairs={{1,0},{2,1},{3,2},{4,3},{5,4},{6,5},{7,6},{8,7},{9,8},{10,9},{11,1... | collective-permute-start | bytes 1572872 | tf_op jit(solution)/shard_map/ppermute | solution.py:21
  37.1 18.7 %collective-permute-done.1.sigma = bf16[1,2,2,256,256]{4,3,2,1,0:T(8,128)(2,1)S(1)} collective-permute-done((bf16[1,2,2,256,256]{4,3,2,1,0:T(8,128)(2,1)}, bf16[1,2,2,256,256]{4,3,2,1,0:T(8,128)(2,1)S(1)}, u32[]{:S(2)}, u32[]{:S(2)}) %collective-permute-start.1) | collective-permute-done | bytes 524320 | tf_op jit(solution)/shard_map/ppermute | solution.py:21
  55.8 1.5 %shard_map.74 = bf16[32,2,2,8,256]{4,3,2,1,0:T(8,128)(2,1)} custom-call(f32[4,2,256,256]{3,2,1,0:T(8,128)S(1)} %own.1, bf16[1,4,2,256,256]{4,3,2,1,0:T(8,128)(2,1)S(1)} %copy-done.1, bf16[1,2,2,256,256]{4,3,2,1,0:T(8,128)(2,1)S(1)} %collective-permute-done.1.sigma), custom_call_target="tpu_custom_call" | custom-call | flops 536870912 | bytes 2621440 | tf_op jit(solution)/shard_map/pallas_call | solution.py:186
  57.3 0.0 all-to-all-done
  57.3 10.0 %all-to-all-start.1 = ((bf16[32,2,2,8,256]{4,3,2,1,0:T(8,128)(2,1)}), bf16[32,2,2,8,256]{4,3,2,1,0:T(8,128)(2,1)S(1)}, u32[]{:S(2)}, u32[]{:S(2)}) async-start(bf16[32,2,2,8,256]{4,3,2,1,0:T(8,128)(2,1)} %shard_map.74), calls=%async_computation.1 | async-start | bytes 1048576 | tf_op jit(solution)/shard_map/all_to_all | solution.py:199
  67.3 0.0 copy-start.4
  67.3 0.0 copy-start.5
  67.3 0.0 copy-start.6
  67.3 1.2 reshape.12
  68.6 0.2 copy.11.early
  68.7 16.6 %all-to-all-done.1 = bf16[32,2,2,8,256]{4,3,2,1,0:T(8,128)(2,1)S(1)} async-done(((bf16[32,2,2,8,256]{4,3,2,1,0:T(8,128)(2,1)}), bf16[32,2,2,8,256]{4,3,2,1,0:T(8,128)(2,1)S(1)}, u32[]{:S(2)}, u32[]{:S(2)}) %all-to-all-start.1) | async-done | bytes 524320 | tf_op jit(solution)/shard_map/all_to_all | solution.py:199
  85.3 0.1 reshape.13
  85.4 0.2 copy.12.late
  85.6 0.0 copy-done.4
  85.6 0.0 copy-done.5
  85.6 0.0 copy-done.6
  85.6 1.7 %correlate.1 = bf16[2,128,2048]{2,1,0:T(8,128)(2,1)S(1)} custom-call(bf16[256,256]{1,0:T(8,128)(2,1)S(1)} %copy-done.4, bf16[128,256]{1,0:T(8,128)(2,1)S(1)} %copy-done.6, bf16[128,256]{1,0:T(8,128)(2,1)S(1)} %copy-done.5, bf16[2,64,2048]{2,1,0:T(8,128)(2,1)S(1)} %copy.11.early, bf16[2,64,2048]{2,1,0:T(8,128)(2,1)S(1)} %copy.12.late), custom_call_target="tpu_custom_call" | custom-call | flops 1073741824 | bytes 2097152 | tf_op jit(solution)/shard_map/correlate/pallas_call | solution.py:209
  87.4 0.3 copy.14
  87.7 0.0 copy-start.3
  87.7 0.1 copy.13
  87.8 34.1 %all_to_all.15.polar = bf16[32,4,2,8,256]{4,3,2,1,0:T(8,128)(2,1)S(1)} all-to-all(bf16[32,4,2,8,256]{4,3,2,1,0:T(8,128)(2,1)S(1)} %copy.13), channel_id=1, replica_groups=mesh['energy'=32,'cuts'=16] {'energy'}, dimensions={0} | all-to-all | bytes 2097152 | tf_op jit(solution)/shard_map/all_to_all | solution.py:221
  121.9 0.0 copy-done.3
  121.9 2.3 %final.1 = bf16[1,4,2,256,256]{4,3,2,1,0:T(8,128)(2,1)} custom-call(bf16[1,4,2,256,256]{4,3,2,1,0:T(8,128)(2,1)S(1)} %copy-done.3, bf16[32,4,2,8,256]{4,3,2,1,0:T(8,128)(2,1)S(1)} %all_to_all.15.polar), custom_call_target="tpu_custom_call" | custom-call | flops 1073741824 | bytes 3145728 | tf_op jit(solution)/shard_map/final/pallas_call | solution.py:223
Async XLA Ops:
  0.0 5.3 %copy-start = (bf16[1,4,2,256,256]{4,3,2,1,0:T(8,128)(2,1)S(1)}, bf16[1,4,2,256,256]{4,3,2,1,0:T(8,128)(2,1)}, u32[]{:S(2)}) copy-start(bf16[1,4,2,256,256]{4,3,2,1,0:T(8,128)(2,1)} %sigma.1) | copy-start | bytes 3145732
  0.0 5.3 %copy-start.2 = (bf16[1,4,2,256,256]{4,3,2,1,0:T(8,128)(2,1)S(1)}, bf16[1,4,2,256,256]{4,3,2,1,0:T(8,128)(2,1)}, u32[]{:S(2)}) copy-start(bf16[1,4,2,256,256]{4,3,2,1,0:T(8,128)(2,1)} %green.3) | copy-start | bytes 3145732
  2.2 16.9 %copy-start.1 = (bf16[1,4,2,256,256]{4,3,2,1,0:T(8,128)(2,1)S(1)}, bf16[1,4,2,256,256]{4,3,2,1,0:T(8,128)(2,1)}, u32[]{:S(2)}) copy-start(bf16[1,4,2,256,256]{4,3,2,1,0:T(8,128)(2,1)} %green.5) | copy-start | bytes 3145732
  2.2 16.9 %collective-permute-start = (bf16[1,2,2,256,256]{4,3,2,1,0:T(8,128)(2,1)S(1)}, bf16[1,2,2,256,256]{4,3,2,1,0:T(8,128)(2,1)S(1)}, u32[]{:S(2)}, u32[]{:S(2)}) collective-permute-start(bf16[1,2,2,256,256]{4,3,2,1,0:T(8,128)(2,1)S(1)} %get-tuple-element.6), channel_id=1, source_target_pairs={{1,0},{2,1},{3,2},{4,3},{5,4},{6,5},{7,6},{8,7},{9,8},{10,9},{11,1... | collective-permute-start | bytes 1572872 | tf_op jit(solution)/shard_map/ppermute | solution.py:21
  20.7 36.7 %all-to-all-start = ((bf16[32,2,2,8,256]{4,3,2,1,0:T(8,128)(2,1)}), bf16[32,2,2,8,256]{4,3,2,1,0:T(8,128)(2,1)}, u32[]{:S(2)}, u32[]{:S(2)}) async-start(bf16[32,2,2,8,256]{4,3,2,1,0:T(8,128)(2,1)} %shard_map.73), calls=%async_computation | async-start | bytes 1048576 | tf_op jit(solution)/shard_map/all_to_all | solution.py:199
  35.2 20.7 %collective-permute-start.1 = (bf16[1,2,2,256,256]{4,3,2,1,0:T(8,128)(2,1)}, bf16[1,2,2,256,256]{4,3,2,1,0:T(8,128)(2,1)S(1)}, u32[]{:S(2)}, u32[]{:S(2)}) collective-permute-start(bf16[1,2,2,256,256]{4,3,2,1,0:T(8,128)(2,1)} %get-tuple-element.5), channel_id=1, source_target_pairs={{1,0},{2,1},{3,2},{4,3},{5,4},{6,5},{7,6},{8,7},{9,8},{10,9},{11,1... | collective-permute-start | bytes 1572872 | tf_op jit(solution)/shard_map/ppermute | solution.py:21
  57.3 28.0 %all-to-all-start.1 = ((bf16[32,2,2,8,256]{4,3,2,1,0:T(8,128)(2,1)}), bf16[32,2,2,8,256]{4,3,2,1,0:T(8,128)(2,1)S(1)}, u32[]{:S(2)}, u32[]{:S(2)}) async-start(bf16[32,2,2,8,256]{4,3,2,1,0:T(8,128)(2,1)} %shard_map.74), calls=%async_computation.1 | async-start | bytes 1048576 | tf_op jit(solution)/shard_map/all_to_all | solution.py:199
  67.3 18.3 %copy-start.4 = (bf16[256,256]{1,0:T(8,128)(2,1)S(1)}, bf16[256,256]{1,0:T(8,128)(2,1)}, u32[]{:S(2)}) copy-start(bf16[256,256]{1,0:T(8,128)(2,1)} %constant.6.clone.forward) | copy-start | bytes 393220
  67.3 18.3 %copy-start.5 = (bf16[128,256]{1,0:T(8,128)(2,1)S(1)}, bf16[128,256]{1,0:T(8,128)(2,1)}, u32[]{:S(2)}) copy-start(bf16[128,256]{1,0:T(8,128)(2,1)} %constant.8.clone.inverse_odd) | copy-start | bytes 196612
  67.3 18.3 %copy-start.6 = (bf16[128,256]{1,0:T(8,128)(2,1)S(1)}, bf16[128,256]{1,0:T(8,128)(2,1)}, u32[]{:S(2)}) copy-start(bf16[128,256]{1,0:T(8,128)(2,1)} %constant.7.clone.inverse_even) | copy-start | bytes 196612
  87.7 34.2 %copy-start.3 = (bf16[1,4,2,256,256]{4,3,2,1,0:T(8,128)(2,1)S(1)}, bf16[1,4,2,256,256]{4,3,2,1,0:T(8,128)(2,1)}, u32[]{:S(2)}) copy-start(bf16[1,4,2,256,256]{4,3,2,1,0:T(8,128)(2,1)} %screening.1) | copy-start | bytes 3145732

commit v3 on v2

--- a/solution.py
+++ b/solution.py
@@ -8,7 +8,6 @@
 from jax.experimental import pallas as pl
 from jax.experimental.pallas import tpu as pltpu
 from jax.sharding import PartitionSpec as P
-
 
 F32 = jnp.float32
 BF16 = jnp.bfloat16
@@ -95,11 +94,11 @@
                 out[0, j, part, side * rows : (side + 1) * rows] = parts[part].astype(BF16)
 
 
-def correlate_kernel(forward, inverse_even, inverse_odd, early, late, out):
+def correlate_kernel(forward, inverse_even, inverse_odd, entries, out):
     count = out.shape[1]
 
     def spectrum(part):
-        data = jnp.concatenate([early[part], late[part]], axis=0)
+        data = entries[part]
         return jnp.dot(forward[...], jnp.concatenate([data, data], axis=0), preferred_element_type=F32)
 
     real, imag = spectrum(0), spectrum(1)
@@ -121,14 +120,13 @@
     return np.concatenate([upper, lower], axis=1)
 
 
-def tables(energies, order):
+def tables(energies):
     period = 2 * energies
     index = np.arange(energies)
-    angle = 2.0 * math.pi / period * (np.outer(index, order) % period)
+    angle = 2.0 * math.pi / period * (np.outer(index, index) % period)
     even, odd = np.cos(angle), np.sin(angle)
-    odd[0] = np.where(order % 2 == 0, 1.0, -1.0)
+    odd[0] = np.where(index % 2 == 0, 1.0, -1.0)
     forward = split_table(np.concatenate([even, odd], axis=0))
-    angle = 2.0 * math.pi / period * (np.outer(index, index) % period)
     scale = 1.0 / (period * energies)
     cos_inv, sin_inv = 2.0 * scale * np.cos(angle), np.sin(angle)
     cos_inv[:, 0] = scale
@@ -166,10 +164,7 @@
     def rows_spec(start=0):
         return pl.BlockSpec((devices, CHUNK, 2, group, size), lambda j: (0, j + start, 0, 0, 0))
 
-    sigma_next = []
-    for index in range(chunks):
-        part = sigma_lesser[:, index * CHUNK : (index + 1) * CHUNK]
-        sigma_next.append(shifted(part, "cuts", -1))
+    sigma_next = shifted(sigma_lesser, "cuts", -1)
     own = pl.pallas_call(
         own_kernel,
         grid=(chunks,),
@@ -180,43 +175,32 @@
         cost_estimate=cost(local * unit, local * plane * 8),
         name="own",
     )(green_diag, sigma_lesser)
-
-    pieces = []
-    for index in range(chunks):
-        lesser = pl.pallas_call(
-            pair_kernel,
-            grid=(1,),
-            in_specs=[
-                own_spec(index),
-                pl.BlockSpec(blocks, lambda j, index=index: (0, j + index, 0, 0, 0)),
-                pl.BlockSpec(blocks, each),
-            ],
-            out_specs=rows_spec(),
-            out_shape=pltpu.HBM((devices, CHUNK, 2, group, size), BF16),
-            compiler_params=params(),
-            cost_estimate=cost(CHUNK * unit, CHUNK * plane * 10),
-        )(own, green_upper, sigma_next[index])
-        piece = lax.all_to_all(lesser, "energy", split_axis=0, concat_axis=0, tiled=True)
-        pieces.append(
-            piece.transpose(2, 0, 1, 3, 4).reshape(2, devices * CHUNK, group * size)
-        )
-
-    grid = np.arange(energies).reshape(devices, chunks, CHUNK)
-    order = grid.transpose(1, 0, 2).reshape(-1)
-    constants = [jnp.asarray(table) for table in tables(energies, order)]
+    lesser = pl.pallas_call(
+        pair_kernel,
+        grid=(chunks,),
+        in_specs=[own_spec(0), pl.BlockSpec(blocks, each), pl.BlockSpec(blocks, each)],
+        out_specs=rows_spec(),
+        out_shape=jax.ShapeDtypeStruct((devices, local, 2, group, size), BF16),
+        compiler_params=params(),
+        cost_estimate=cost(local * unit, local * plane * 10),
+        name="pair",
+    )(own, green_upper, sigma_next)
+    entries = lax.all_to_all(lesser, "energy", split_axis=0, concat_axis=0, tiled=True)
+    entries = entries.transpose(2, 0, 1, 3, 4).reshape(2, energies, group * size)
+    constants = [jnp.asarray(table) for table in tables(energies)]
     width = group * size
     step = width // 2
     polar = pl.pallas_call(
         correlate_kernel,
         grid=(width // step,),
         in_specs=[pl.BlockSpec(table.shape, lambda i: (0, 0)) for table in constants]
-        + [pl.BlockSpec((2, piece.shape[1], step), lambda i: (0, 0, i)) for piece in pieces],
+        + [pl.BlockSpec((2, energies, step), lambda i: (0, 0, i))],
         out_specs=pl.BlockSpec((2, energies, step), lambda i: (0, 0, i)),
         out_shape=jax.ShapeDtypeStruct((2, energies, width), BF16),
         compiler_params=params(),
         cost_estimate=cost(2 * 2 * 256 * 256 * width * 2, energies * width * 8),
         name="correlate",
-    )(*constants, *pieces)
+    )(*constants, entries)
     rows = polar.transpose(1, 0, 2).reshape(devices, local, 2, group, size)
     field = lax.all_to_all(rows, "energy", split_axis=0, concat_axis=0, tiled=True)
 

time: 125 us -> 112 us (0.90)
  blocking collectives: 34.1 us -> 76 us
  starting transfers between devices: 29.5 us -> 3.1 us
  waiting for transfers between devices: 47.7 us -> 21.4 us
  Pallas kernels: 8.53 us -> 6.99 us
    all_to_all x0 -> x1, blocking collectives: none -> 42.4 us  [shards(): lax.all_to_all(lesser, 'energy', split_axis=0, concat_axis=0, tiled=True)]
    all_to_all x2 -> x0, starting transfers between devices: 24.5 us -> none  [shards(): lax.all_to_all(lesser, 'energy', split_axis=0, concat_axis=0, tiled=True)]
    all_to_all x2 -> x0, waiting for transfers between devices: 16.6 us -> none  [shards(): lax.all_to_all(lesser, 'energy', split_axis=0, concat_axis=0, tiled=True)]
    ppermute x2 -> x1, waiting for transfers between devices: 31.1 us -> 21.4 us  [shifted(): lax.ppermute(value, axis, [(source, source + steps) for source in range(l...]
    unnamed x15, local copies, waits for them, and re-layouts: 0.34 us -> 3.05 us
    slice x1 -> x0, local copies, waits for them, and re-layouts: 2.21 us -> none  [shards(): part = sigma_lesser[:, index * CHUNK:(index + 1) * CHUNK]]
    ppermute x2 -> x1, starting transfers between devices: 5.02 us -> 3.1 us  [shifted(): lax.ppermute(value, axis, [(source, source + steps) for source in range(l...]
    pallas_call x2 -> x1, Pallas kernels: 3.01 us -> 1.51 us  [shards(): pl.pallas_call(pair_kernel, grid=(chunks,), in_specs=[own_spec(0), pl.Blo...]
  transfers between devices with their start and end apart: 4 -> 1, of which waited for: 3 -> 1; matrix products, arithmetic and copies ran while one was open for 1% -> 0% of each run, Pallas kernels for 2% -> 1%
where the time goes in v3:
time: 112 us; the launch traced here: 111 us
  blocking collectives  76 us (68%)
  waiting for transfers between devices  21.4 us (19%)
  Pallas kernels  6.99 us (6%)
  local copies, waits for them, and re-layouts  3.75 us (3%)
  starting transfers between devices  3.1 us (3%)
    all_to_all x1, blocking collectives, shards(): lax.all_to_all(lesser, 'energy', split_axis=0, concat_axis=0, tiled=True)  42.4 us
    all_to_all x1, blocking collectives, shards(): lax.all_to_all(rows, 'energy', split_axis=0, concat_axis=0, tiled=True)  33.7 us
    ppermute x1, waiting for transfers between devices, shifted(): lax.ppermute(value, axis, [(source, source + steps) for source in range(l...  21.4 us
    ppermute x1, starting transfers between devices, shifted(): lax.ppermute(value, axis, [(source, source + steps) for source in range(l...  3.1 us
    unnamed x15, local copies, waits for them, and re-layouts  3.05 us
    pallas_call x1, Pallas kernels, shards(): pl.pallas_call(final_kernel, grid=(chunks,), in_specs=[pl.BlockSpec(block...  2.33 us
  transfers between devices with their start and end apart: 1, of which 1 were waited for; matrix products, arithmetic and copies ran while one was open for 0% of the time, Pallas kernels for 1%

profile of v3, /device:TPU:57, one launch (start us, length us, event | category | flops | bytes accessed | tf_op | source)
XLA Modules:
  0.0 111.3 jit_solution(4404983568884241518)
XLA Ops:
  0.0 0.0 copy-start
  0.0 3.1 %collective-permute-start = (bf16[1,4,2,256,256]{4,3,2,1,0:T(8,128)(2,1)}, bf16[1,4,2,256,256]{4,3,2,1,0:T(8,128)(2,1)S(1)}, u32[]{:S(2)}, u32[]{:S(2)}) collective-permute-start(bf16[1,4,2,256,256]{4,3,2,1,0:T(8,128)(2,1)} %sigma.1), channel_id=1, source_target_pairs={{1,0},{2,1},{3,2},{4,3},{5,4},{6,5},{7,6},{8,7},{9,8},{10,9},{11,1... | collective-permute-start | bytes 3145736 | tf_op jit(solution)/shard_map/ppermute | solution.py:20
  3.1 0.0 copy-start.1
  3.1 1.2 %copy-done.1 = bf16[1,4,2,256,256]{4,3,2,1,0:T(8,128)(2,1)S(1)} copy-done((bf16[1,4,2,256,256]{4,3,2,1,0:T(8,128)(2,1)S(1)}, bf16[1,4,2,256,256]{4,3,2,1,0:T(8,128)(2,1)}, u32[]{:S(2)}) %copy-start.1) | copy-done | bytes 1048600
  4.3 0.0 copy-start.2
  4.3 1.2 %copy-done.2 = bf16[1,4,2,256,256]{4,3,2,1,0:T(8,128)(2,1)S(1)} copy-done((bf16[1,4,2,256,256]{4,3,2,1,0:T(8,128)(2,1)S(1)}, bf16[1,4,2,256,256]{4,3,2,1,0:T(8,128)(2,1)}, u32[]{:S(2)}) %copy-start.2) | copy-done | bytes 1048600
  5.6 1.4 %own.1 = f32[4,2,256,256]{3,2,1,0:T(8,128)S(1)} custom-call(bf16[1,4,2,256,256]{4,3,2,1,0:T(8,128)(2,1)S(1)} %copy-done.1, bf16[1,4,2,256,256]{4,3,2,1,0:T(8,128)(2,1)S(1)} %copy-done.2), custom_call_target="tpu_custom_call" | custom-call | flops 1073741824 | bytes 4194304 | tf_op jit(solution)/shard_map/own/pallas_call | solution.py:168
  7.0 21.4 %collective-permute-done.sigma = bf16[1,4,2,256,256]{4,3,2,1,0:T(8,128)(2,1)S(1)} collective-permute-done((bf16[1,4,2,256,256]{4,3,2,1,0:T(8,128)(2,1)}, bf16[1,4,2,256,256]{4,3,2,1,0:T(8,128)(2,1)S(1)}, u32[]{:S(2)}, u32[]{:S(2)}) %collective-permute-start) | collective-permute-done | bytes 1048608 | tf_op jit(solution)/shard_map/ppermute | solution.py:20
  28.4 0.0 copy-done
  28.4 1.5 %pair.1 = bf16[32,4,2,8,256]{4,3,2,1,0:T(8,128)(2,1)S(1)} custom-call(f32[4,2,256,256]{3,2,1,0:T(8,128)S(1)} %own.1, bf16[1,4,2,256,256]{4,3,2,1,0:T(8,128)(2,1)S(1)} %copy-done, bf16[1,4,2,256,256]{4,3,2,1,0:T(8,128)(2,1)S(1)} %collective-permute-done.sigma), custom_call_target="tpu_custom_call" | custom-call | flops 1073741824 | bytes 5242880 | tf_op jit(solution)/shard_map/pair/pallas_call | solution.py:178
  29.9 42.4 %all_to_all.10 = bf16[32,4,2,8,256]{4,3,2,1,0:T(8,128)(2,1)S(1)} all-to-all(bf16[32,4,2,8,256]{4,3,2,1,0:T(8,128)(2,1)S(1)} %pair.1), channel_id=1, replica_groups=mesh['energy'=32,'cuts'=16] {'energy'}, dimensions={0} | all-to-all | bytes 2097152 | tf_op jit(solution)/shard_map/all_to_all | solution.py:188
  72.3 0.0 copy-start.4
  72.3 0.0 copy-start.5
  72.3 0.0 copy-start.6
  72.3 0.3 reshape.8
  72.5 0.4 copy.10.entries
  72.9 0.3 copy-done.4
  73.2 0.0 copy-done.5
  73.2 0.0 copy-done.6
  73.2 1.7 %correlate.1 = bf16[2,128,2048]{2,1,0:T(8,128)(2,1)S(1)} custom-call(bf16[256,256]{1,0:T(8,128)(2,1)S(1)} %copy-done.4, bf16[128,256]{1,0:T(8,128)(2,1)S(1)} %copy-done.6, bf16[128,256]{1,0:T(8,128)(2,1)S(1)} %copy-done.5, bf16[2,128,2048]{2,1,0:T(8,128)(2,1)S(1)} %copy.10.entries), custom_call_target="tpu_custom_call" | custom-call | flops 1073741824 | bytes 2097152 | tf_op jit(solution)/shard_map/correlate/pallas_call | solution.py:193
  74.9 0.3 copy.12
  75.2 0.0 copy-start.3
  75.2 0.1 copy.11
  75.3 33.7 %all_to_all.11.polar = bf16[32,4,2,8,256]{4,3,2,1,0:T(8,128)(2,1)S(1)} all-to-all(bf16[32,4,2,8,256]{4,3,2,1,0:T(8,128)(2,1)S(1)} %copy.11), channel_id=1, replica_groups=mesh['energy'=32,'cuts'=16] {'energy'}, dimensions={0} | all-to-all | bytes 2097152 | tf_op jit(solution)/shard_map/all_to_all | solution.py:205
  109.0 0.0 copy-done.3
  109.0 2.3 %final.1 = bf16[1,4,2,256,256]{4,3,2,1,0:T(8,128)(2,1)} custom-call(bf16[1,4,2,256,256]{4,3,2,1,0:T(8,128)(2,1)S(1)} %copy-done.3, bf16[32,4,2,8,256]{4,3,2,1,0:T(8,128)(2,1)S(1)} %all_to_all.11.polar), custom_call_target="tpu_custom_call" | custom-call | flops 1073741824 | bytes 3145728 | tf_op jit(solution)/shard_map/final/pallas_call | solution.py:207
Async XLA Ops:
  0.0 28.4 %copy-start = (bf16[1,4,2,256,256]{4,3,2,1,0:T(8,128)(2,1)S(1)}, bf16[1,4,2,256,256]{4,3,2,1,0:T(8,128)(2,1)}, u32[]{:S(2)}) copy-start(bf16[1,4,2,256,256]{4,3,2,1,0:T(8,128)(2,1)} %green.3) | copy-start | bytes 3145732
  0.0 28.4 %collective-permute-start = (bf16[1,4,2,256,256]{4,3,2,1,0:T(8,128)(2,1)}, bf16[1,4,2,256,256]{4,3,2,1,0:T(8,128)(2,1)S(1)}, u32[]{:S(2)}, u32[]{:S(2)}) collective-permute-start(bf16[1,4,2,256,256]{4,3,2,1,0:T(8,128)(2,1)} %sigma.1), channel_id=1, source_target_pairs={{1,0},{2,1},{3,2},{4,3},{5,4},{6,5},{7,6},{8,7},{9,8},{10,9},{11,1... | collective-permute-start | bytes 3145736 | tf_op jit(solution)/shard_map/ppermute | solution.py:20
  3.1 1.2 %copy-start.1 = (bf16[1,4,2,256,256]{4,3,2,1,0:T(8,128)(2,1)S(1)}, bf16[1,4,2,256,256]{4,3,2,1,0:T(8,128)(2,1)}, u32[]{:S(2)}) copy-start(bf16[1,4,2,256,256]{4,3,2,1,0:T(8,128)(2,1)} %green.2) | copy-start | bytes 3145732
  4.3 1.2 %copy-start.2 = (bf16[1,4,2,256,256]{4,3,2,1,0:T(8,128)(2,1)S(1)}, bf16[1,4,2,256,256]{4,3,2,1,0:T(8,128)(2,1)}, u32[]{:S(2)}) copy-start(bf16[1,4,2,256,256]{4,3,2,1,0:T(8,128)(2,1)} %sigma.1) | copy-start | bytes 3145732
  72.3 0.9 copy-start.4
  72.3 0.9 copy-start.5
  72.3 0.9 copy-start.6
  75.2 33.8 %copy-start.3 = (bf16[1,4,2,256,256]{4,3,2,1,0:T(8,128)(2,1)S(1)}, bf16[1,4,2,256,256]{4,3,2,1,0:T(8,128)(2,1)}, u32[]{:S(2)}) copy-start(bf16[1,4,2,256,256]{4,3,2,1,0:T(8,128)(2,1)} %screening.1) | copy-start | bytes 3145732

commit v4 on v3

--- a/solution.py
+++ b/solution.py
@@ -94,14 +94,14 @@
                 out[0, j, part, side * rows : (side + 1) * rows] = parts[part].astype(BF16)
 
 
-def correlate_kernel(forward, inverse_even, inverse_odd, entries, out):
+def correlate_kernel(forward, inverse_even, inverse_odd, reals, imags, out):
     count = out.shape[1]
 
     def spectrum(part):
-        data = entries[part]
+        data = part[...]
         return jnp.dot(forward[...], jnp.concatenate([data, data], axis=0), preferred_element_type=F32)
 
-    real, imag = spectrum(0), spectrum(1)
+    real, imag = spectrum(reals), spectrum(imags)
     even_real, odd_real = real[:count], real[count:]
     even_imag, odd_imag = imag[:count], imag[count:]
     even = even_real * even_real + even_imag * even_imag
@@ -186,7 +186,7 @@
         name="pair",
     )(own, green_upper, sigma_next)
     entries = lax.all_to_all(lesser, "energy", split_axis=0, concat_axis=0, tiled=True)
-    entries = entries.transpose(2, 0, 1, 3, 4).reshape(2, energies, group * size)
+    entries = entries.reshape(energies, 2 * group * size)
     constants = [jnp.asarray(table) for table in tables(energies)]
     width = group * size
     step = width // 2
@@ -194,13 +194,16 @@
         correlate_kernel,
         grid=(width // step,),
         in_specs=[pl.BlockSpec(table.shape, lambda i: (0, 0)) for table in constants]
-        + [pl.BlockSpec((2, energies, step), lambda i: (0, 0, i))],
+        + [
+            pl.BlockSpec((energies, step), lambda i: (0, i)),
+            pl.BlockSpec((energies, step), lambda i: (0, i + width // step)),
+        ],
         out_specs=pl.BlockSpec((2, energies, step), lambda i: (0, 0, i)),
         out_shape=jax.ShapeDtypeStruct((2, energies, width), BF16),
         compiler_params=params(),
         cost_estimate=cost(2 * 2 * 256 * 256 * width * 2, energies * width * 8),
         name="correlate",
-    )(*constants, entries)
+    )(*constants, entries, entries)
     rows = polar.transpose(1, 0, 2).reshape(devices, local, 2, group, size)
     field = lax.all_to_all(rows, "energy", split_axis=0, concat_axis=0, tiled=True)
 

time: 112 us -> 111 us (level)
  no operation moved by 1% of the time
where the time goes in v4:
time: 111 us
  blocking collectives  76.1 us (69%)
  waiting for transfers between devices  21.4 us (19%)
  Pallas kernels  7.02 us (6%)
  local copies, waits for them, and re-layouts  3.36 us (3%)
  starting transfers between devices  3.1 us (3%)
    all_to_all x1, blocking collectives, shards(): lax.all_to_all(lesser, 'energy', split_axis=0, concat_axis=0, tiled=True)  42.5 us
    all_to_all x1, blocking collectives, shards(): lax.all_to_all(rows, 'energy', split_axis=0, concat_axis=0, tiled=True)  33.6 us
    ppermute x1, waiting for transfers between devices, shifted(): lax.ppermute(value, axis, [(source, source + steps) for source in range(l...  21.4 us
    ppermute x1, starting transfers between devices, shifted(): lax.ppermute(value, axis, [(source, source + steps) for source in range(l...  3.1 us
    unnamed x15, local copies, waits for them, and re-layouts  2.77 us
    pallas_call x1, Pallas kernels, shards(): pl.pallas_call(final_kernel, grid=(chunks,), in_specs=[pl.BlockSpec(block...  2.33 us
  transfers between devices with their start and end apart: 1, of which 1 were waited for; matrix products, arithmetic and copies ran while one was open for 0% of the time, Pallas kernels for 1%

profile of v4, /device:TPU:57, one launch (start us, length us, event | category | flops | bytes accessed | tf_op | source)
XLA Modules:
  0.0 111.1 jit_solution(13942569964445495684)
XLA Ops:
  0.0 0.0 copy-start
  0.0 3.1 %collective-permute-start = (bf16[1,4,2,256,256]{4,3,2,1,0:T(8,128)(2,1)}, bf16[1,4,2,256,256]{4,3,2,1,0:T(8,128)(2,1)S(1)}, u32[]{:S(2)}, u32[]{:S(2)}) collective-permute-start(bf16[1,4,2,256,256]{4,3,2,1,0:T(8,128)(2,1)} %sigma.1), channel_id=1, source_target_pairs={{1,0},{2,1},{3,2},{4,3},{5,4},{6,5},{7,6},{8,7},{9,8},{10,9},{11,1... | collective-permute-start | bytes 3145736 | tf_op jit(solution)/shard_map/ppermute | solution.py:20
  3.1 0.0 copy-start.1
  3.1 1.2 %copy-done.1 = bf16[1,4,2,256,256]{4,3,2,1,0:T(8,128)(2,1)S(1)} copy-done((bf16[1,4,2,256,256]{4,3,2,1,0:T(8,128)(2,1)S(1)}, bf16[1,4,2,256,256]{4,3,2,1,0:T(8,128)(2,1)}, u32[]{:S(2)}) %copy-start.1) | copy-done | bytes 1048600
  4.3 0.0 copy-start.2
  4.3 1.2 %copy-done.2 = bf16[1,4,2,256,256]{4,3,2,1,0:T(8,128)(2,1)S(1)} copy-done((bf16[1,4,2,256,256]{4,3,2,1,0:T(8,128)(2,1)S(1)}, bf16[1,4,2,256,256]{4,3,2,1,0:T(8,128)(2,1)}, u32[]{:S(2)}) %copy-start.2) | copy-done | bytes 1048600
  5.6 1.4 %own.1 = f32[4,2,256,256]{3,2,1,0:T(8,128)S(1)} custom-call(bf16[1,4,2,256,256]{4,3,2,1,0:T(8,128)(2,1)S(1)} %copy-done.1, bf16[1,4,2,256,256]{4,3,2,1,0:T(8,128)(2,1)S(1)} %copy-done.2), custom_call_target="tpu_custom_call" | custom-call | flops 1073741824 | bytes 4194304 | tf_op jit(solution)/shard_map/own/pallas_call | solution.py:168
  7.0 21.4 %collective-permute-done.sigma = bf16[1,4,2,256,256]{4,3,2,1,0:T(8,128)(2,1)S(1)} collective-permute-done((bf16[1,4,2,256,256]{4,3,2,1,0:T(8,128)(2,1)}, bf16[1,4,2,256,256]{4,3,2,1,0:T(8,128)(2,1)S(1)}, u32[]{:S(2)}, u32[]{:S(2)}) %collective-permute-start) | collective-permute-done | bytes 1048608 | tf_op jit(solution)/shard_map/ppermute | solution.py:20
  28.4 0.0 copy-done
  28.4 1.5 %pair.1 = bf16[32,4,2,8,256]{4,3,2,1,0:T(8,128)(2,1)S(1)} custom-call(f32[4,2,256,256]{3,2,1,0:T(8,128)S(1)} %own.1, bf16[1,4,2,256,256]{4,3,2,1,0:T(8,128)(2,1)S(1)} %copy-done, bf16[1,4,2,256,256]{4,3,2,1,0:T(8,128)(2,1)S(1)} %collective-permute-done.sigma), custom_call_target="tpu_custom_call" | custom-call | flops 1073741824 | bytes 5242880 | tf_op jit(solution)/shard_map/pair/pallas_call | solution.py:178
  29.9 0.0 copy-start.4
  29.9 0.0 copy-start.5
  29.9 0.0 copy-start.6
  29.9 42.5 %all_to_all.10 = bf16[32,4,2,8,256]{4,3,2,1,0:T(8,128)(2,1)S(1)} all-to-all(bf16[32,4,2,8,256]{4,3,2,1,0:T(8,128)(2,1)S(1)} %pair.1), channel_id=1, replica_groups=mesh['energy'=32,'cuts'=16] {'energy'}, dimensions={0} | all-to-all | bytes 2097152 | tf_op jit(solution)/shard_map/all_to_all | solution.py:188
  72.4 0.5 reshape.6.reals.imags
  72.9 0.0 copy-done.4
  73.0 0.0 copy-done.5
  73.0 0.0 copy-done.6
  73.0 1.7 %correlate.1 = bf16[2,128,2048]{2,1,0:T(8,128)(2,1)S(1)} custom-call(bf16[256,256]{1,0:T(8,128)(2,1)S(1)} %copy-done.4, bf16[128,256]{1,0:T(8,128)(2,1)S(1)} %copy-done.6, bf16[128,256]{1,0:T(8,128)(2,1)S(1)} %copy-done.5, bf16[128,4096]{1,0:T(8,128)(2,1)S(1)} %reshape.6.reals.imags, bf16[128,4096]{1,0:T(8,128)(2,1)S(1)} %reshape.6.reals.imags), custom_call_target="tpu_custom_call" | custom-call | flops 1073741824 | bytes 2097152 | tf_op jit(solution)/shard_map/correlate/pallas_call | solution.py:193
  74.7 0.3 copy.10
  75.0 0.0 copy-start.3
  75.0 0.1 copy.9
  75.1 33.6 %all_to_all.11.polar = bf16[32,4,2,8,256]{4,3,2,1,0:T(8,128)(2,1)S(1)} all-to-all(bf16[32,4,2,8,256]{4,3,2,1,0:T(8,128)(2,1)S(1)} %copy.9), channel_id=1, replica_groups=mesh['energy'=32,'cuts'=16] {'energy'}, dimensions={0} | all-to-all | bytes 2097152 | tf_op jit(solution)/shard_map/all_to_all | solution.py:208
  108.8 0.0 copy-done.3
  108.8 2.3 %final.1 = bf16[1,4,2,256,256]{4,3,2,1,0:T(8,128)(2,1)} custom-call(bf16[1,4,2,256,256]{4,3,2,1,0:T(8,128)(2,1)S(1)} %copy-done.3, bf16[32,4,2,8,256]{4,3,2,1,0:T(8,128)(2,1)S(1)} %all_to_all.11.polar), custom_call_target="tpu_custom_call" | custom-call | flops 1073741824 | bytes 3145728 | tf_op jit(solution)/shard_map/final/pallas_call | solution.py:210
Async XLA Ops:
  0.0 28.4 %copy-start = (bf16[1,4,2,256,256]{4,3,2,1,0:T(8,128)(2,1)S(1)}, bf16[1,4,2,256,256]{4,3,2,1,0:T(8,128)(2,1)}, u32[]{:S(2)}) copy-start(bf16[1,4,2,256,256]{4,3,2,1,0:T(8,128)(2,1)} %green.3) | copy-start | bytes 3145732
  0.0 28.4 %collective-permute-start = (bf16[1,4,2,256,256]{4,3,2,1,0:T(8,128)(2,1)}, bf16[1,4,2,256,256]{4,3,2,1,0:T(8,128)(2,1)S(1)}, u32[]{:S(2)}, u32[]{:S(2)}) collective-permute-start(bf16[1,4,2,256,256]{4,3,2,1,0:T(8,128)(2,1)} %sigma.1), channel_id=1, source_target_pairs={{1,0},{2,1},{3,2},{4,3},{5,4},{6,5},{7,6},{8,7},{9,8},{10,9},{11,1... | collective-permute-start | bytes 3145736 | tf_op jit(solution)/shard_map/ppermute | solution.py:20
  3.1 1.2 %copy-start.1 = (bf16[1,4,2,256,256]{4,3,2,1,0:T(8,128)(2,1)S(1)}, bf16[1,4,2,256,256]{4,3,2,1,0:T(8,128)(2,1)}, u32[]{:S(2)}) copy-start(bf16[1,4,2,256,256]{4,3,2,1,0:T(8,128)(2,1)} %green.2) | copy-start | bytes 3145732
  4.3 1.2 %copy-start.2 = (bf16[1,4,2,256,256]{4,3,2,1,0:T(8,128)(2,1)S(1)}, bf16[1,4,2,256,256]{4,3,2,1,0:T(8,128)(2,1)}, u32[]{:S(2)}) copy-start(bf16[1,4,2,256,256]{4,3,2,1,0:T(8,128)(2,1)} %sigma.1) | copy-start | bytes 3145732
  29.9 43.0 %copy-start.4 = (bf16[256,256]{1,0:T(8,128)(2,1)S(1)}, bf16[256,256]{1,0:T(8,128)(2,1)}, u32[]{:S(2)}) copy-start(bf16[256,256]{1,0:T(8,128)(2,1)} %constant.6.clone.forward) | copy-start | bytes 393220
  29.9 43.0 %copy-start.5 = (bf16[128,256]{1,0:T(8,128)(2,1)S(1)}, bf16[128,256]{1,0:T(8,128)(2,1)}, u32[]{:S(2)}) copy-start(bf16[128,256]{1,0:T(8,128)(2,1)} %constant.8.clone.inverse_odd) | copy-start | bytes 196612
  29.9 43.0 %copy-start.6 = (bf16[128,256]{1,0:T(8,128)(2,1)S(1)}, bf16[128,256]{1,0:T(8,128)(2,1)}, u32[]{:S(2)}) copy-start(bf16[128,256]{1,0:T(8,128)(2,1)} %constant.7.clone.inverse_even) | copy-start | bytes 196612
  75.0 33.7 %copy-start.3 = (bf16[1,4,2,256,256]{4,3,2,1,0:T(8,128)(2,1)S(1)}, bf16[1,4,2,256,256]{4,3,2,1,0:T(8,128)(2,1)}, u32[]{:S(2)}) copy-start(bf16[1,4,2,256,256]{4,3,2,1,0:T(8,128)(2,1)} %screening.1) | copy-start | bytes 3145732

commit v5 on v4

v5 whole, which is shorter than its diff:
```python
import functools
import math

import jax
import jax.numpy as jnp
import numpy as np
from jax import lax
from jax.experimental import pallas as pl
from jax.experimental.pallas import tpu as pltpu
from jax.sharding import PartitionSpec as P


F32 = jnp.float32
BF16 = jnp.bfloat16
FIRST, MIDDLE = 1, 3


def moved(value, pairs):
    return lax.ppermute(value, "cuts", pairs)


def product(left, right):
    rows = left.shape[0] // 2
    by_real = jnp.dot(left, right[0], preferred_element_type=F32)
    by_imag = jnp.dot(left, right[1], preferred_element_type=F32)
    return by_real[:rows] - by_imag[rows:], by_real[rows:] + by_imag[:rows]


def product_adjoint(left, right):
    rows = left.shape[0] // 2
    turned = functools.partial(
        lax.dot_general, dimension_numbers=(((1,), (1,)), ((), ())), preferred_element_type=F32
    )
    by_real = turned(left, right[0])
    by_imag = turned(left, right[1])
    return by_real[:rows] + by_imag[rows:], by_real[rows:] - by_imag[:rows]


def pair_of(ref, j):
    return ref[0, j, 0], ref[0, j, 1]


def joined(pair):
    return jnp.concatenate([part.astype(BF16) for part in pair], axis=0)


def halves(ref, j):
    rows = ref.shape[-2] // 2
    return [
        jnp.concatenate([ref[0, j, part, start : start + rows] for part in range(2)], axis=0)
        for start in (0, rows)
    ]


def sandwich(outer, inner):
    count = outer.shape[1]
    terms = [
        [joined(product(half, inner(j))) for half in halves(outer, j)] for j in range(count)
    ]
    return [[product_adjoint(term, pair_of(outer, j)) for term in terms[j]] for j in range(count)]


def own_kernel(green, sigma, out):
    rows = out.shape[-2] // 2
    (sides,) = sandwich(green, lambda j: pair_of(sigma, j))
    for side, parts in enumerate(sides):
        for part in range(2):
            out[0, part, side * rows : (side + 1) * rows] = parts[part]


def store_lesser(own, green, sigma, out):
    devices, group, size = out.shape[0], out.shape[3], out.shape[4]
    rows, half = size // 2, devices // 2
    (sides,) = sandwich(green, lambda j: sigma)
    for side, parts in enumerate(sides):
        for part in range(2):
            total = parts[part] + own[0, part, side * rows : (side + 1) * rows]
            out[side * half : (side + 1) * half, 0, part] = total.astype(BF16).reshape(half, group, size)


def plain_kernel(own, green, sigma, out):
    store_lesser(own, green, pair_of(sigma, 0), out)


def last_kernel(own, green, within, crossed, _, out):
    sigma = tuple(within[0, 0, part] + crossed[0, 0, part] for part in range(2))
    store_lesser(own, green, sigma, out)


def final_kernel(screening, polar, out):
    size = out.shape[-1]
    rows = size // 2

    def inner(j):
        return tuple(polar[:, j, part].reshape(size, size) for part in range(2))

    for j, sides in enumerate(sandwich(screening, inner)):
        for side, parts in enumerate(sides):
            for part in range(2):
                out[0, j, part, side * rows : (side + 1) * rows] = parts[part].astype(BF16)


def correlate_kernel(forward, inverse_even, inverse_odd, *rest):
    *parts, out = rest
    count = out.shape[1]

    def spectrum(early, late):
        data = jnp.concatenate([early[...], late[...]], axis=0)
        return jnp.dot(forward[...], jnp.concatenate([data, data], axis=0), preferred_element_type=F32)

    real, imag = spectrum(*parts[:2]), spectrum(*parts[2:])
    even_real, odd_real = real[:count], real[count:]
    even_imag, odd_imag = imag[:count], imag[count:]
    even = even_real * even_real + even_imag * even_imag
    odd = odd_real * odd_real + odd_imag * odd_imag
    cross = (even_real * odd_imag - even_imag * odd_real).astype(BF16)
    power = jnp.concatenate([even.astype(BF16), odd.astype(BF16)], axis=0)
    out[0] = jnp.dot(inverse_even[...], power, preferred_element_type=F32).astype(BF16)
    out[1] = jnp.dot(
        inverse_odd[...], jnp.concatenate([cross, cross], axis=0), preferred_element_type=F32
    ).astype(BF16)


def split_table(table):
    upper = table.astype(jnp.bfloat16)
    lower = (table - upper.astype(np.float64)).astype(jnp.bfloat16)
    return np.concatenate([upper, lower], axis=1)


def tables(energies, order):
    period = 2 * energies
    index = np.arange(energies)
    angle = 2.0 * math.pi / period * (np.outer(index, order) % period)
    even, odd = np.cos(angle), np.sin(angle)
    odd[0] = np.where(order % 2 == 0, 1.0, -1.0)
    forward = split_table(np.concatenate([even, odd], axis=0))
    angle = 2.0 * math.pi / period * (np.outer(index, index) % period)
    scale = 1.0 / (period * energies)
    cos_inv, sin_inv = 2.0 * scale * np.cos(angle), np.sin(angle)
    cos_inv[:, 0] = scale
    nyquist = cos_inv.copy()
    nyquist[:, 0] = scale * np.where(index % 2 == 0, 1.0, -1.0)
    inverse_even = np.concatenate([cos_inv, nyquist], axis=1).astype(jnp.bfloat16)
    inverse_odd = split_table(4.0 * scale * sin_inv)
    return forward, inverse_even, inverse_odd


def params(mebibytes=20):
    return pltpu.CompilerParams(vmem_limit_bytes=mebibytes * 2**20)


def cost(flops, accessed):
    return pl.CostEstimate(flops=flops, bytes_accessed=accessed, transcendentals=0)


def shards(green_diag, green_upper, sigma_lesser, screening):
    local, size = green_diag.shape[1], green_diag.shape[-1]
    devices, cuts = lax.axis_size("energy"), lax.axis_size("cuts")
    energies = local * devices
    group = size // devices
    unit = 16 * size**3
    plane = 2 * size * size
    one = (1, 1, 2, size, size)
    single = (1, 2, size, size)

    def energy(start=0):
        return pl.BlockSpec(one, lambda j: (0, j + start, 0, 0, 0))

    half = cuts // 2
    direct = [(s + 1, s) for s in range(cuts - 1)]
    across = (half, half - 1)
    within = [pair for pair in direct if pair != across]
    next_first = moved(sigma_lesser[:, :FIRST], direct)
    next_middle = moved(sigma_lesser[:, FIRST:MIDDLE], direct)
    sigma_last = lax.optimization_barrier(sigma_lesser)[:, MIDDLE:]
    next_last = moved(sigma_last, within)
    crossed = moved(sigma_last, [across])

    def own_of(start, stop):
        return pl.pallas_call(
            own_kernel,
            grid=(stop - start,),
            in_specs=[energy(start), energy(start)],
            out_specs=pl.BlockSpec(single, lambda j: (j, 0, 0, 0)),
            out_shape=jax.ShapeDtypeStruct((stop - start, 2, size, size), F32),
            compiler_params=params(),
            cost_estimate=cost((stop - start) * unit, (stop - start) * plane * 8),
        )(*(pltpu.with_memory_space_constraint(a, pltpu.HBM) for a in (green_diag, sigma_lesser)))

    own_first = own_of(0, FIRST)
    own_rest = own_of(FIRST, local)

    def lesser_of(kernel, own, start, stop, into, sigmas, buffer=None):
        count = stop - start
        base = start if own is own_first else start - FIRST
        whole = [] if buffer is None else [buffer]
        total = FIRST if own is own_first else local - FIRST
        return pl.pallas_call(
            kernel,
            grid=(count,),
            in_specs=[pl.BlockSpec(single, lambda j: (j + base, 0, 0, 0)), energy(start)]
            + [energy()] * len(sigmas)
            + [pl.BlockSpec(memory_space=pl.ANY)] * len(whole),
            out_specs=pl.BlockSpec((devices, 1, 2, group, size), lambda j: (0, j + into, 0, 0, 0)),
            out_shape=pltpu.HBM((devices, total, 2, group, size), BF16),
            input_output_aliases={2 + len(sigmas): 0} if whole else {},
            compiler_params=params(),
            cost_estimate=cost(count * unit, count * plane * 10),
        )(own, green_upper, *sigmas, *whole)

    def exchanged(value):
        return lax.all_to_all(value, "energy", split_axis=0, concat_axis=0, tiled=True)

    early = exchanged(lesser_of(plain_kernel, own_first, 0, FIRST, 0, [next_first]))
    rest = lesser_of(plain_kernel, own_rest, FIRST, MIDDLE, 0, [next_middle])
    sigmas = [next_last, crossed]
    rest = lesser_of(last_kernel, own_rest, MIDDLE, local, MIDDLE - FIRST, sigmas, rest)
    late = exchanged(rest)
    pieces = [piece.reshape(-1, 2 * group * size) for piece in (early, late)]

    grid = np.arange(energies).reshape(devices, local)
    order = np.concatenate([grid[:, :FIRST].reshape(-1), grid[:, FIRST:].reshape(-1)])
    constants = [jnp.asarray(table) for table in tables(energies, order)]
    width = group * size
    step = width // 2
    polar = pl.pallas_call(
        correlate_kernel,
        grid=(width // step,),
        in_specs=[pl.BlockSpec(table.shape, lambda i: (0, 0)) for table in constants]
        + [
            pl.BlockSpec((piece.shape[0], step), lambda i, start=start: (0, i + start))
            for start in (0, width // step)
            for piece in pieces
        ],
        out_specs=pl.BlockSpec((2, energies, step), lambda i: (0, 0, i)),
        out_shape=jax.ShapeDtypeStruct((2, energies, width), BF16),
        compiler_params=params(),
        cost_estimate=cost(2 * 2 * 256 * 256 * width * 2, energies * width * 8),
        name="correlate",
    )(*constants, *pieces, *pieces)
    field = exchanged(polar.transpose(1, 0, 2).reshape(devices, local, 2, group, size))

    pair = 2
    return pl.pallas_call(
        final_kernel,
        grid=(local // pair,),
        in_specs=[
            pl.BlockSpec((1, pair, 2, size, size), lambda j: (0, j, 0, 0, 0)),
            pl.BlockSpec((devices, pair, 2, group, size), lambda j: (0, j, 0, 0, 0)),
        ],
        out_specs=pl.BlockSpec((1, pair, 2, size, size), lambda j: (0, j, 0, 0, 0)),
        out_shape=jax.ShapeDtypeStruct(screening.shape, BF16),
        compiler_params=params(),
        cost_estimate=cost(local * unit, local * plane * 6),
        name="final",
    )(screening, field)


def solution(mesh):
    spec = P("cuts", "energy", None, None, None)
    return jax.shard_map(
        shards, mesh=mesh, in_specs=(spec, spec, spec, spec), out_specs=spec, check_vma=False
    )
```

time: 111 us -> 114 us (1.027); the launches traced: 111 us -> 113 us
  blocking collectives: 76.1 us -> 33.8 us
  starting transfers between devices: 3.1 us -> 34.9 us
  Pallas kernels: 7.02 us -> 13.1 us
  waiting for transfers between devices: 21.4 us -> 26.8 us
    all_to_all x2 -> x1, blocking collectives: 76.1 us -> 33.8 us  [exchanged(): lax.all_to_all(value, 'energy', split_axis=0, concat_axis=0, tiled=True)]
    all_to_all x0 -> x2, starting transfers between devices: none -> 26.2 us  [exchanged(): lax.all_to_all(value, 'energy', split_axis=0, concat_axis=0, tiled=True)]
    all_to_all x0 -> x2, waiting for transfers between devices: none -> 19 us  [exchanged(): lax.all_to_all(value, 'energy', split_axis=0, concat_axis=0, tiled=True)]
    ppermute x1 -> x4, waiting for transfers between devices: 21.4 us -> 7.74 us  [moved(): return lax.ppermute(value, 'cuts', pairs)]
    pallas_call x3 -> x6, Pallas kernels: 5.28 us -> 11.4 us  [the longest x2 4.74 us: own_of(): pl.pallas_call(own_kernel, grid=(stop - start,), in_specs=[energy(start),...]
    ppermute x1 -> x4, starting transfers between devices: 3.1 us -> 8.68 us  [moved(): return lax.ppermute(value, 'cuts', pairs)]
    slice x0 -> x3, local copies, waits for them, and re-layouts: none -> 3.02 us  [the longest x1 1.08 us: shards(): next_middle = moved(sigma_lesser[:, FIRST:MIDDLE], direct)]
    unnamed x15 -> x12, local copies, waits for them, and re-layouts: 2.77 us -> 0.41 us
  transfers between devices with their start and end apart: 1 -> 6, of which waited for: 1 -> 3; matrix products, arithmetic and copies ran while one was open for 0% -> 2% of each run, Pallas kernels for 1% -> 8%
where the time goes in v5:
time: 114 us; the launch traced here: 113 us
  starting transfers between devices  34.9 us (31%)
  blocking collectives  33.8 us (30%)
  waiting for transfers between devices  26.8 us (24%)
  Pallas kernels  13.1 us (11%)
  local copies, waits for them, and re-layouts  3.87 us (3%)
    all_to_all x1, blocking collectives, exchanged(): lax.all_to_all(value, 'energy', split_axis=0, concat_axis=0, tiled=True)  33.8 us
    all_to_all x2, starting transfers between devices, exchanged(): lax.all_to_all(value, 'energy', split_axis=0, concat_axis=0, tiled=True)  26.2 us
    all_to_all x2, waiting for transfers between devices, exchanged(): lax.all_to_all(value, 'energy', split_axis=0, concat_axis=0, tiled=True)  19 us
    ppermute x4, starting transfers between devices, moved(): return lax.ppermute(value, 'cuts', pairs)  8.68 us
    ppermute x4, waiting for transfers between devices, moved(): return lax.ppermute(value, 'cuts', pairs)  7.74 us
    pallas_call x2, Pallas kernels, own_of(): pl.pallas_call(own_kernel, grid=(stop - start,), in_specs=[energy(start),...  4.74 us
    pallas_call x3, Pallas kernels, lesser_of(): pl.pallas_call(kernel, grid=(count,), in_specs=[pl.BlockSpec(single, lamb...  4.33 us
    pallas_call x1, Pallas kernels, shards(): pl.pallas_call(final_kernel, grid=(local // pair,), in_specs=[pl.BlockSpe...  2.33 us
  transfers between devices with their start and end apart: 6, of which 3 were waited for; matrix products, arithmetic and copies ran while one was open for 2% of the time, Pallas kernels for 8%

profile of v5, /device:TPU:57, one launch (start us, length us, event | category | flops | bytes accessed | tf_op | source)
XLA Modules:
  0.0 112.6 jit_solution(1198904974237566958)
XLA Ops:
  0.0 1.0 slice.9
  1.0 3.0 %collective-permute-start = (bf16[1,1,2,256,256]{4,3,2,1,0:T(8,128)(2,1)S(1)}, bf16[1,1,2,256,256]{4,3,2,1,0:T(8,128)(2,1)S(1)}, u32[]{:S(2)}, u32[]{:S(2)}) collective-permute-start(bf16[1,1,2,256,256]{4,3,2,1,0:T(8,128)(2,1)S(1)} %slice.9), channel_id=1, source_target_pairs={{1,0},{2,1},{3,2},{4,3},{5,4},{6,5},{7,6},{8,7},{9,8},{10,9},{11,1... | collective-permute-start | bytes 786440 | tf_op jit(solution)/shard_map/ppermute | solution.py:19
  4.0 1.1 slice.11
  5.0 0.0 copy-start
  5.0 3.1 %collective-permute-start.3 = (bf16[1,2,2,256,256]{4,3,2,1,0:T(8,128)(2,1)S(1)}, bf16[1,2,2,256,256]{4,3,2,1,0:T(8,128)(2,1)S(1)}, u32[]{:S(2)}, u32[]{:S(2)}) collective-permute-start(bf16[1,2,2,256,256]{4,3,2,1,0:T(8,128)(2,1)S(1)} %slice.11), channel_id=1, source_target_pairs={{1,0},{2,1},{3,2},{4,3},{5,4},{6,5},{7,6},{8,7},{9,8},{10,9},{11,1... | collective-permute-start | bytes 1572872 | tf_op jit(solution)/shard_map/ppermute | solution.py:19
  8.2 1.6 %shard_map.73.own = f32[1,2,256,256]{3,2,1,0:T(8,128)S(1)} custom-call(bf16[1,4,2,256,256]{4,3,2,1,0:T(8,128)(2,1)} %green.7, bf16[1,4,2,256,256]{4,3,2,1,0:T(8,128)(2,1)} %sigma.3), custom_call_target="tpu_custom_call" | custom-call | flops 268435456 | bytes 1048576 | tf_op jit(solution)/shard_map/pallas_call | solution.py:180
  9.7 2.4 %collective-permute-done.sigma = bf16[1,1,2,256,256]{4,3,2,1,0:T(8,128)(2,1)S(1)} collective-permute-done((bf16[1,1,2,256,256]{4,3,2,1,0:T(8,128)(2,1)S(1)}, bf16[1,1,2,256,256]{4,3,2,1,0:T(8,128)(2,1)S(1)}, u32[]{:S(2)}, u32[]{:S(2)}) %collective-permute-start) | collective-permute-done | bytes 262176 | tf_op jit(solution)/shard_map/ppermute | solution.py:19
  12.2 0.0 copy-done
  12.2 1.2 %shard_map.74 = bf16[32,1,2,8,256]{4,3,2,1,0:T(8,128)(2,1)} custom-call(f32[1,2,256,256]{3,2,1,0:T(8,128)S(1)} %shard_map.73.own, bf16[1,4,2,256,256]{4,3,2,1,0:T(8,128)(2,1)S(1)} %copy-done, bf16[1,1,2,256,256]{4,3,2,1,0:T(8,128)(2,1)S(1)} %collective-permute-done.sigma), custom_call_target="tpu_custom_call" | custom-call | flops 268435456 | bytes 1310720 | tf_op jit(solution)/shard_map/pallas_call | solution.py:198
  13.4 15.6 %all-to-all-start = ((bf16[32,1,2,8,256]{4,3,2,1,0:T(8,128)(2,1)}), bf16[32,1,2,8,256]{4,3,2,1,0:T(8,128)(2,1)S(1)}, u32[]{:S(2)}, u32[]{:S(2)}) async-start(bf16[32,1,2,8,256]{4,3,2,1,0:T(8,128)(2,1)} %shard_map.74), calls=%async_computation | async-start | bytes 524288 | tf_op jit(solution)/shard_map/all_to_all | solution.py:212
  29.0 1.0 slice.12
  30.0 1.3 %collective-permute-start.1 = (bf16[1,1,2,256,256]{4,3,2,1,0:T(8,128)(2,1)S(1)}, bf16[1,1,2,256,256]{4,3,2,1,0:T(8,128)(2,1)S(1)}, u32[]{:S(2)}, u32[]{:S(2)}) collective-permute-start(bf16[1,1,2,256,256]{4,3,2,1,0:T(8,128)(2,1)S(1)} %slice.12), channel_id=1, source_target_pairs={{1,0},{2,1},{3,2},{4,3},{5,4},{6,5},{7,6},{9,8},{10,9},{11,10},{12... | collective-permute-start | bytes 786440 | tf_op jit(solution)/shard_map/ppermute | solution.py:19
  31.3 1.3 %collective-permute-start.2 = (bf16[1,1,2,256,256]{4,3,2,1,0:T(8,128)(2,1)S(1)}, bf16[1,1,2,256,256]{4,3,2,1,0:T(8,128)(2,1)S(1)}, u32[]{:S(2)}, u32[]{:S(2)}) collective-permute-start(bf16[1,1,2,256,256]{4,3,2,1,0:T(8,128)(2,1)S(1)} %slice.12), channel_id=1, source_target_pairs={{8,7},{24,23},{40,39},{56,55},{72,71},{88,87},{104,103},{120,119},... | collective-permute-start | bytes 786440 | tf_op jit(solution)/shard_map/ppermute | solution.py:19
  32.6 3.2 %shard_map.75.own = f32[3,2,256,256]{3,2,1,0:T(8,128)S(1)} custom-call(bf16[1,4,2,256,256]{4,3,2,1,0:T(8,128)(2,1)} %green.7, bf16[1,4,2,256,256]{4,3,2,1,0:T(8,128)(2,1)} %sigma.3), custom_call_target="tpu_custom_call" | custom-call | flops 805306368 | bytes 3145728 | tf_op jit(solution)/shard_map/pallas_call | solution.py:180
  35.8 0.0 collective-permute-done.3.sigma
  35.8 1.8 %shard_map.76._ = bf16[32,3,2,8,256]{4,3,2,1,0:T(8,128)(2,1)} custom-call(f32[3,2,256,256]{3,2,1,0:T(8,128)S(1)} %shard_map.75.own, bf16[1,4,2,256,256]{4,3,2,1,0:T(8,128)(2,1)S(1)} %copy-done, bf16[1,2,2,256,256]{4,3,2,1,0:T(8,128)(2,1)S(1)} %collective-permute-done.3.sigma), custom_call_target="tpu_custom_call" | custom-call | flops 536870912 | bytes 2621440 | tf_op jit(solution)/shard_map/pallas_call | solution.py:198
  37.6 0.0 collective-permute-done.1.within
  37.6 5.3 %collective-permute-done.2.crossed = bf16[1,1,2,256,256]{4,3,2,1,0:T(8,128)(2,1)S(1)} collective-permute-done((bf16[1,1,2,256,256]{4,3,2,1,0:T(8,128)(2,1)S(1)}, bf16[1,1,2,256,256]{4,3,2,1,0:T(8,128)(2,1)S(1)}, u32[]{:S(2)}, u32[]{:S(2)}) %collective-permute-start.2) | collective-permute-done | bytes 262176 | tf_op jit(solution)/shard_map/ppermute | solution.py:19
  42.9 1.2 %shard_map.77 = bf16[32,3,2,8,256]{4,3,2,1,0:T(8,128)(2,1)} custom-call(f32[3,2,256,256]{3,2,1,0:T(8,128)S(1)} %shard_map.75.own, bf16[1,4,2,256,256]{4,3,2,1,0:T(8,128)(2,1)S(1)} %copy-done, bf16[1,1,2,256,256]{4,3,2,1,0:T(8,128)(2,1)S(1)} %collective-permute-done.1.within, ...), custom_call_target="tpu_custom_call", output_to_operand_aliasing={{}: (4, {})} | custom-call | flops 268435456 | bytes 1310720 | tf_op jit(solution)/shard_map/pallas_call | solution.py:198
  44.2 0.0 copy-start.2
  44.2 0.0 copy-start.3
  44.2 0.0 copy-start.4
  44.2 0.0 all-to-all-done
  44.2 10.6 %all-to-all-start.1 = ((bf16[32,3,2,8,256]{4,3,2,1,0:T(8,128)(2,1)}), bf16[32,3,2,8,256]{4,3,2,1,0:T(8,128)(2,1)S(1)}, u32[]{:S(2)}, u32[]{:S(2)}) async-start(bf16[32,3,2,8,256]{4,3,2,1,0:T(8,128)(2,1)} %shard_map.77), calls=%async_computation.1 | async-start | bytes 1572864 | tf_op jit(solution)/shard_map/all_to_all | solution.py:212
  54.8 0.1 copy.11
  54.9 19.0 %all-to-all-done.1 = bf16[32,3,2,8,256]{4,3,2,1,0:T(8,128)(2,1)S(1)} async-done(((bf16[32,3,2,8,256]{4,3,2,1,0:T(8,128)(2,1)}), bf16[32,3,2,8,256]{4,3,2,1,0:T(8,128)(2,1)S(1)}, u32[]{:S(2)}, u32[]{:S(2)}) %all-to-all-start.1) | async-done | bytes 786464 | tf_op jit(solution)/shard_map/all_to_all | solution.py:212
  73.9 0.4 reshape.10.rest_1_.rest_3_
  74.3 0.0 copy-done.2
  74.3 0.0 copy-done.3
  74.3 0.0 copy-done.4
  74.3 1.8 %correlate.1 = bf16[2,128,2048]{2,1,0:T(8,128)(2,1)S(1)} custom-call(bf16[256,256]{1,0:T(8,128)(2,1)S(1)} %copy-done.2, bf16[128,256]{1,0:T(8,128)(2,1)S(1)} %copy-done.3, bf16[128,256]{1,0:T(8,128)(2,1)S(1)} %copy-done.4, bf16[32,4096]{1,0:T(8,128)(2,1)S(1)} %bitcast.13, bf16[96,4096]{1,0:T(8,128)(2,1)S(1)} %reshape.10.rest_1_.rest_3_, ...), custom_call_target="tpu_custom_call" | custom-call | flops 1073741824 | bytes 2097152 | tf_op jit(solution)/shard_map/correlate/pallas_call | solution.py:226
  76.1 0.3 copy.12
  76.4 0.1 copy.10
  76.5 0.0 copy-start.1
  76.5 33.8 %all_to_all.15.polar = bf16[32,4,2,8,256]{4,3,2,1,0:T(8,128)(2,1)S(1)} all-to-all(bf16[32,4,2,8,256]{4,3,2,1,0:T(8,128)(2,1)S(1)} %copy.10), channel_id=1, replica_groups=mesh['energy'=32,'cuts'=16] {'energy'}, dimensions={0} | all-to-all | bytes 2097152 | tf_op jit(solution)/shard_map/all_to_all | solution.py:212
  110.3 0.0 copy-done.1
  110.3 2.3 %final.1 = bf16[1,4,2,256,256]{4,3,2,1,0:T(8,128)(2,1)} custom-call(bf16[1,4,2,256,256]{4,3,2,1,0:T(8,128)(2,1)S(1)} %copy-done.1, bf16[32,4,2,8,256]{4,3,2,1,0:T(8,128)(2,1)S(1)} %all_to_all.15.polar), custom_call_target="tpu_custom_call" | custom-call | flops 1073741824 | bytes 3145728 | tf_op jit(solution)/shard_map/final/pallas_call | solution.py:244
Async XLA Ops:
  1.0 11.2 %collective-permute-start = (bf16[1,1,2,256,256]{4,3,2,1,0:T(8,128)(2,1)S(1)}, bf16[1,1,2,256,256]{4,3,2,1,0:T(8,128)(2,1)S(1)}, u32[]{:S(2)}, u32[]{:S(2)}) collective-permute-start(bf16[1,1,2,256,256]{4,3,2,1,0:T(8,128)(2,1)S(1)} %slice.9), channel_id=1, source_target_pairs={{1,0},{2,1},{3,2},{4,3},{5,4},{6,5},{7,6},{8,7},{9,8},{10,9},{11,1... | collective-permute-start | bytes 786440 | tf_op jit(solution)/shard_map/ppermute | solution.py:19
  5.0 7.1 %copy-start = (bf16[1,4,2,256,256]{4,3,2,1,0:T(8,128)(2,1)S(1)}, bf16[1,4,2,256,256]{4,3,2,1,0:T(8,128)(2,1)}, u32[]{:S(2)}) copy-start(bf16[1,4,2,256,256]{4,3,2,1,0:T(8,128)(2,1)} %green.9) | copy-start | bytes 3145732
  5.0 30.7 %collective-permute-start.3 = (bf16[1,2,2,256,256]{4,3,2,1,0:T(8,128)(2,1)S(1)}, bf16[1,2,2,256,256]{4,3,2,1,0:T(8,128)(2,1)S(1)}, u32[]{:S(2)}, u32[]{:S(2)}) collective-permute-start(bf16[1,2,2,256,256]{4,3,2,1,0:T(8,128)(2,1)S(1)} %slice.11), channel_id=1, source_target_pairs={{1,0},{2,1},{3,2},{4,3},{5,4},{6,5},{7,6},{8,7},{9,8},{10,9},{11,1... | collective-permute-start | bytes 1572872 | tf_op jit(solution)/shard_map/ppermute | solution.py:19
  13.4 30.8 %all-to-all-start = ((bf16[32,1,2,8,256]{4,3,2,1,0:T(8,128)(2,1)}), bf16[32,1,2,8,256]{4,3,2,1,0:T(8,128)(2,1)S(1)}, u32[]{:S(2)}, u32[]{:S(2)}) async-start(bf16[32,1,2,8,256]{4,3,2,1,0:T(8,128)(2,1)} %shard_map.74), calls=%async_computation | async-start | bytes 524288 | tf_op jit(solution)/shard_map/all_to_all | solution.py:212
  30.0 7.6 %collective-permute-start.1 = (bf16[1,1,2,256,256]{4,3,2,1,0:T(8,128)(2,1)S(1)}, bf16[1,1,2,256,256]{4,3,2,1,0:T(8,128)(2,1)S(1)}, u32[]{:S(2)}, u32[]{:S(2)}) collective-permute-start(bf16[1,1,2,256,256]{4,3,2,1,0:T(8,128)(2,1)S(1)} %slice.12), channel_id=1, source_target_pairs={{1,0},{2,1},{3,2},{4,3},{5,4},{6,5},{7,6},{9,8},{10,9},{11,10},{12... | collective-permute-start | bytes 786440 | tf_op jit(solution)/shard_map/ppermute | solution.py:19
  31.3 11.6 %collective-permute-start.2 = (bf16[1,1,2,256,256]{4,3,2,1,0:T(8,128)(2,1)S(1)}, bf16[1,1,2,256,256]{4,3,2,1,0:T(8,128)(2,1)S(1)}, u32[]{:S(2)}, u32[]{:S(2)}) collective-permute-start(bf16[1,1,2,256,256]{4,3,2,1,0:T(8,128)(2,1)S(1)} %slice.12), channel_id=1, source_target_pairs={{8,7},{24,23},{40,39},{56,55},{72,71},{88,87},{104,103},{120,119},... | collective-permute-start | bytes 786440 | tf_op jit(solution)/shard_map/ppermute | solution.py:19
  44.2 30.1 %copy-start.2 = (bf16[256,256]{1,0:T(8,128)(2,1)S(1)}, bf16[256,256]{1,0:T(8,128)(2,1)}, u32[]{:S(2)}) copy-start(bf16[256,256]{1,0:T(8,128)(2,1)} %constant.6.clone.forward) | copy-start | bytes 393220
  44.2 30.1 %copy-start.3 = (bf16[128,256]{1,0:T(8,128)(2,1)S(1)}, bf16[128,256]{1,0:T(8,128)(2,1)}, u32[]{:S(2)}) copy-start(bf16[128,256]{1,0:T(8,128)(2,1)} %constant.7.clone.inverse_even) | copy-start | bytes 196612
  44.2 30.1 %copy-start.4 = (bf16[128,256]{1,0:T(8,128)(2,1)S(1)}, bf16[128,256]{1,0:T(8,128)(2,1)}, u32[]{:S(2)}) copy-start(bf16[128,256]{1,0:T(8,128)(2,1)} %constant.8.clone.inverse_odd) | copy-start | bytes 196612
  44.2 29.7 %all-to-all-start.1 = ((bf16[32,3,2,8,256]{4,3,2,1,0:T(8,128)(2,1)}), bf16[32,3,2,8,256]{4,3,2,1,0:T(8,128)(2,1)S(1)}, u32[]{:S(2)}, u32[]{:S(2)}) async-start(bf16[32,3,2,8,256]{4,3,2,1,0:T(8,128)(2,1)} %shard_map.77), calls=%async_computation.1 | async-start | bytes 1572864 | tf_op jit(solution)/shard_map/all_to_all | solution.py:212
  76.5 33.8 %copy-start.1 = (bf16[1,4,2,256,256]{4,3,2,1,0:T(8,128)(2,1)S(1)}, bf16[1,4,2,256,256]{4,3,2,1,0:T(8,128)(2,1)}, u32[]{:S(2)}) copy-start(bf16[1,4,2,256,256]{4,3,2,1,0:T(8,128)(2,1)} %screening.1) | copy-start | bytes 3145732
